TPU v7x, 32 devices: a whole 2x2x4 slice. The times are simulated.
32 devices in a mesh: dp: 8 (over y, x, core), fsdp: 4 (over z).
Axes of the slice: x: 2, y: 2, z: 4, core: 2. Of those that a mesh axis runs over, the one named last changes fastest.
Arguments:
- cells_in: bfloat16 [32, 1024, 768], P(('dp', 'fsdp')), may hold values from -6 to 6
- out_grad: bfloat16 [32, 1024, 768], P(('dp', 'fsdp')), may hold values from -6 to 6
- cell_length: int32 [32], replicated, may hold values from 300 to 1024, as said below
- cell_place: int32 [32], replicated, may hold values from 0 to 31, each once
- gene_ids: int32 [32, 1024], P(('dp', 'fsdp')), may hold values from 0 to 35999
- attn_norm_gain: bfloat16 [768], P('fsdp'), may hold values from 0.5 to 1.5
- attn_norm_bias: bfloat16 [768], P('fsdp'), may hold values from -3 to 3
- query_weight: bfloat16 [768, 768], P('fsdp'), may hold values from -0.21875 to 0.21875
- query_bias: bfloat16 [768], P('fsdp'), may hold values from -3 to 3
- key_weight: bfloat16 [768, 768], P('fsdp'), may hold values from -0.21875 to 0.21875
- value_weight: bfloat16 [768, 768], P('fsdp'), may hold values from -0.21875 to 0.21875
- value_bias: bfloat16 [768], P('fsdp'), may hold values from -3 to 3
- out_weight: bfloat16 [768, 768], P('fsdp'), may hold values from -1.75 to 1.75
- out_bias: bfloat16 [768], P('fsdp'), may hold values from -3 to 3
- ffn_norm_gain: bfloat16 [768], P('fsdp'), may hold values from 0.5 to 1.5
- ffn_norm_bias: bfloat16 [768], P('fsdp'), may hold values from -3 to 3
- up_weight: bfloat16 [768, 3072], P('fsdp'), may hold values from -0.21875 to 0.21875
- up_bias: bfloat16 [3072], P('fsdp'), may hold values from -3 to 3
- down_weight: bfloat16 [3072, 768], P('fsdp'), may hold values from -0.109375 to 0.109375
- down_bias: bfloat16 [768], P('fsdp'), may hold values from -3 to 3
Outputs:
- block_out: bfloat16 [32, 1024, 768], P(('dp', 'fsdp'))
- input_grad: bfloat16 [32, 1024, 768], P(('dp', 'fsdp'))
- grad_attn_norm_gain: float32 [768], P('fsdp')
- grad_attn_norm_bias: float32 [768], P('fsdp')
- grad_query_weight: float32 [768, 768], P('fsdp')
- grad_query_bias: float32 [768], P('fsdp')
- grad_key_weight: float32 [768, 768], P('fsdp')
- grad_value_weight: float32 [768, 768], P('fsdp')
- grad_value_bias: float32 [768], P('fsdp')
- grad_out_weight: float32 [768, 768], P('fsdp')
- grad_out_bias: float32 [768], P('fsdp')
- grad_ffn_norm_gain: float32 [768], P('fsdp')
- grad_ffn_norm_bias: float32 [768], P('fsdp')
- grad_up_weight: float32 [768, 3072], P('fsdp')
- grad_up_bias: float32 [3072], P('fsdp')
- grad_down_weight: float32 [3072, 768], P('fsdp')
- grad_down_bias: float32 [768], P('fsdp')
- gene_counts: int32 [36000], replicated
Inputs may be any that keep to these rules, and one draw needn't show every extreme that they name: `cell_length`: every cell has 300 to 1024 live genes; in every draw one cell has exactly 1024 and another exactly 300. `cell_place`: each cell number appears once.
All inputs are finite; a program needn't handle non-finite values.
Results may differ from a plain program's by a relative error of at most 0.017.
Values may be sent and summed in bfloat16 or wider, within the bound.
No kernel may reach another device: no remote copies, remote signals or barrier semaphores. Data moves between devices by JAX's collectives and lax.ppermute only.
A program may use at most 320 MiB of HBM per device.

v0:
```python
from functools import partial

import jax
import jax.numpy as jnp
from jax import lax
from jax.experimental import pallas as pl
from jax.experimental.pallas import tpu as pltpu
from jax.sharding import PartitionSpec as P

HEADS = 12
HEAD_DIM = 64
VOCAB = 36000
EPSILON = 1e-05
NEGATIVE = -1e30
PAIR = 2 * HEAD_DIM
CHUNK = 1536
TALLY_ROWS = 288

F32 = jnp.float32
BF16 = jnp.bfloat16
VMEM_LIMIT = 60 << 20

GAIN_ONE, SHIFT_ONE, OUT_B, GAIN_TWO, SHIFT_TWO, DOWN_B, QUERY_B, VALUE_B, UP_B = range(9)
SUM_ROWS = 16

WHOLE = pl.BlockSpec(memory_space=pl.ANY)
SCALARS = pl.BlockSpec(memory_space=pltpu.SMEM)


LIGHT = pl.CostEstimate(flops=1024, transcendentals=0, bytes_accessed=1024)


def call(kernel, name, grid, in_specs, out_specs, out_shape, scratch=(), prefetch=0, aliases=None):
    return pl.pallas_call(
        kernel,
        grid_spec=pltpu.PrefetchScalarGridSpec(
            num_scalar_prefetch=prefetch,
            grid=grid,
            in_specs=in_specs,
            out_specs=out_specs,
            scratch_shapes=scratch,
        ),
        out_shape=out_shape,
        input_output_aliases=aliases or {},
        compiler_params=pltpu.CompilerParams(vmem_limit_bytes=VMEM_LIMIT),
        cost_estimate=LIGHT,
        name=name,
    )


def shape(dims, dtype):
    return jax.ShapeDtypeStruct(dims, dtype)


def dot(left, right):
    return jnp.dot(left, right, preferred_element_type=F32)


def dot_nt(left, right):
    return lax.dot_general(left, right, (((1,), (1,)), ((), ())), preferred_element_type=F32)


def dot_tn(left, right):
    return lax.dot_general(left, right, (((0,), (0,)), ((), ())), preferred_element_type=F32)


def moments(values):
    width = values.shape[-1]
    center = values - jnp.sum(values, axis=-1, keepdims=True) * (1.0 / width)
    spread = jnp.sum(center * center, axis=-1, keepdims=True) * (1.0 / width)
    inverse = lax.rsqrt(spread + EPSILON)
    return center * inverse, inverse


def norm_back(grad_out, normed, inverse, gain):
    width = normed.shape[-1]
    scaled = grad_out * gain
    mean = jnp.sum(scaled, axis=-1, keepdims=True) * (1.0 / width)
    along = jnp.sum(scaled * normed, axis=-1, keepdims=True) * (1.0 / width)
    return inverse * (scaled - mean - normed * along)


def start_all(copies):
    for copy in copies:
        copy.start()


def wait_all(copies):
    for copy in copies:
        copy.wait()


def aligned(begin, size, unit):
    return pl.ds(pl.multiple_of(begin, unit), size)


def pack_kernel(slots, where, *refs):
    pairs, (o, up, down), small, (first, rest) = (
        refs[: 3 * slots], refs[3 * slots : 3 * slots + 3], refs[3 * slots + 3 : -2], refs[-2:],
    )
    rows, half = o.shape
    width = down.shape[1]
    for number, ref in enumerate(pairs):
        first[0:rows, number * PAIR : (number + 1) * PAIR] = ref[...]
    first[rows:, :] = jnp.zeros((first.shape[0] - rows, first.shape[1]), BF16)
    for number, ref in enumerate(small):
        value = ref[...].astype(F32).reshape(1, -1).astype(BF16)
        first[rows + number : rows + number + 1, 0 : ref.shape[0]] = value
    row = 0
    for begin in range(0, up.shape[1], width):
        rest[row : row + rows, :] = up[:, begin : begin + width]
        row += rows
    rest[row : row + rows, 0:half] = o[...]
    rest[row : row + rows, half:width] = jnp.zeros((rows, width - half), BF16)
    rest[row + rows :, :] = down[...]


def pack(where, q, k, v, o, up, down, small):
    rows, width = q.shape[0] // 4, q.shape[1]
    slots = width // PAIR // 2
    deep = down.shape[0] // 8
    first = (rows + SUM_ROWS, 3 * PAIR * slots)
    rest = (rows * (up.shape[1] // 2 // width + 1) + deep, width)
    return call(
        partial(pack_kernel, slots),
        "pack",
        (1,),
        [
            pl.BlockSpec((rows, PAIR), lambda i, w, s=slot: (w[1], slots * w[2] + s))
            for slot in range(slots)
            for _ in range(3)
        ]
        + [
            pl.BlockSpec((rows, o.shape[1] // 2), lambda i, w: (w[1], w[2])),
            pl.BlockSpec((rows, up.shape[1] // 2), lambda i, w: (w[1], w[2])),
            pl.BlockSpec((deep, width), lambda i, w: (4 * w[2] + w[1], 0)),
        ]
        + [pl.BlockSpec(part.shape, lambda i, w: (0,)) for part in small],
        [pl.BlockSpec(part, lambda i, w: (0, 0)) for part in (first, rest)],
        [shape(part, BF16) for part in (first, rest)],
        prefetch=1,
    )(where, *([q, k, v] * slots), o, up, down, *small)


def split_kernel(parts, *refs):
    ins, outs = refs[: -len(parts)], refs[-len(parts) :]
    for (row, column), out in zip(parts, outs):
        rows, columns = out.shape[1:]
        for number, ref in enumerate(ins):
            out[number] = ref[row : row + rows, column : column + columns]


def split(arrays, parts):
    full = arrays[0].shape
    return call(
        partial(split_kernel, [part[:2] for part in parts]),
        "split",
        (1,),
        [pl.BlockSpec(full, lambda i: (0, 0))] * len(arrays),
        [pl.BlockSpec((len(arrays), *part[2:]), lambda i: (0, 0, 0)) for part in parts],
        [shape((len(arrays), *part[2:]), BF16) for part in parts],
    )(*arrays)


def sort_kernel(where, gathered, *outs):
    begin = 0
    for out in outs:
        rows = out.shape[1]
        for number in range(out.shape[0]):
            out[number] = gathered[where[0] ^ (number + 1), begin : begin + rows, :]
        begin += rows


def sort(where, gathered, sizes):
    count, _, width = gathered.shape
    return call(
        sort_kernel,
        "sort",
        (1,),
        [SCALARS, pl.BlockSpec(gathered.shape, lambda i: (0, 0, 0))],
        [pl.BlockSpec((count - 1, size, width), lambda i: (0, 0, 0)) for size in sizes],
        [shape((count - 1, size, width), BF16) for size in sizes],
    )(where, gathered)


def remote_places(where, pieces, count):
    z, quad, core = where[0], where[1], where[2]
    for number, piece in enumerate(pieces):
        turn, side = number % 4, number // 4
        for step in range(1, count):
            yield piece, step - 1, z ^ step, quad ^ turn, core ^ side


def pair_copies(where, own, pieces, full, sems, count, slot):
    shard = own[0].shape[0]
    slots = own[0].shape[1] // PAIR // 2
    rows, half = pieces[0].shape[1:]
    copies = []
    for kind, ref in enumerate(own):
        for core in range(2):
            for number in range(half // (3 * PAIR)):
                source = (core * slots + slot + number) * PAIR
                target = core * half + (3 * number + kind) * PAIR
                copies.append(
                    pltpu.make_async_copy(
                        ref.at[:, source : source + PAIR],
                        full.at[aligned(where[0] * shard, shard, 16), target : target + PAIR],
                        sems.at[len(copies)],
                    )
                )
    for piece, step, z, quad, core in remote_places(where, pieces, count):
        copies.append(
            pltpu.make_async_copy(
                piece.at[step],
                full.at[aligned(z * shard + quad * rows, rows, 16), aligned(core * half, half, 128)],
                sems.at[len(copies)],
            )
        )
    return copies


def column_copies(where, own, pieces, full, sems, count, row):
    shard = own.shape[0]
    rows, half = shard // 4, own.shape[1] // 2
    width = pieces[0].shape[2]
    copies = [pltpu.make_async_copy(own, full.at[aligned(where[0] * shard, shard, 16)], sems.at[0])]
    for piece, step, z, quad, core in remote_places(where, pieces, count):
        for number, begin in enumerate(range(0, half, width)):
            size = min(width, half - begin)
            copies.append(
                pltpu.make_async_copy(
                    piece.at[step, row + number * rows : row + (number + 1) * rows, 0:size],
                    full.at[
                        aligned(z * shard + quad * rows, rows, 16),
                        aligned(core * half + begin, size, 128),
                    ],
                    sems.at[len(copies)],
                )
            )
    return copies


def row_copies(where, own, pieces, full, sems, count):
    shard = own.shape[0]
    rows = pieces[0].shape[1]
    copies = [
        pltpu.make_async_copy(own, full.at[aligned(where[0] * shard, shard, 16)], sems.at[0])
    ]
    for piece, step, z, quad, core in remote_places(where, pieces, count):
        copies.append(
            pltpu.make_async_copy(
                piece.at[step],
                full.at[aligned(z * shard + core * 4 * rows + quad * rows, rows, 16)],
                sems.at[len(copies)],
            )
        )
    return copies


def copy_count(count):
    return 1 + 8 * (count - 1)


def norm_kernel(count, shard, where, x_ref, *rest):
    small, (a_ref, t_ref, vec_ref, up_ref, bias_ref) = rest[:count], rest[count:]

    @pl.when(pl.program_id(0) == 0)
    def _():
        wide = up_ref.shape[1] // count
        for owner in range(count):
            value = small[0][...].astype(F32)
            for step in range(1, count):
                here = (where[0] ^ step) == owner
                value = jnp.where(here, small[step][...].astype(F32), value)
            vec_ref[:, owner * shard : (owner + 1) * shard] = value[0:8, 0:shard]
            up_ref[:, owner * wide : (owner + 1) * wide] = value[UP_B : UP_B + 1, 0:wide]
        slots = vec_ref.shape[1] // PAIR // 2
        for core in range(2):
            for slot in range(slots):
                span = slice((core * slots + slot) * PAIR, (core * slots + slot + 1) * PAIR)
                begin = 3 * PAIR * spot(slot, core, slots)
                bias_ref[:, begin : begin + PAIR] = vec_ref[QUERY_B : QUERY_B + 1, span]
                bias_ref[:, begin + PAIR : begin + 2 * PAIR] = jnp.zeros((1, PAIR), F32)
                bias_ref[:, begin + 2 * PAIR : begin + 3 * PAIR] = vec_ref[
                    VALUE_B : VALUE_B + 1, span
                ]

    normed, _ = moments(x_ref[...].astype(F32))
    rows = normed * vec_ref[GAIN_ONE : GAIN_ONE + 1, :] + vec_ref[SHIFT_ONE : SHIFT_ONE + 1, :]
    rows = rows.astype(BF16)
    a_ref[...] = rows
    t_ref[...] = rows.T


def spot(slot, core, slots):
    return jnp.where(slot == 0, core, 1 + core * (slots - 1) + slot) if not isinstance(
        slot, int
    ) else (core if slot == 0 else 1 + core * (slots - 1) + slot)


def first_norm(where, inputs, small, shard, wide, block=512):
    seq, width = inputs.shape
    count = len(small)
    fixed = lambda a, b: pl.BlockSpec((a, b), lambda i: (0, 0))
    last = small[0].shape[0] // SUM_ROWS - 1
    return call(
        partial(norm_kernel, count, shard),
        "first_norm",
        (seq // block,),
        [SCALARS, pl.BlockSpec((block, width), lambda i: (i, 0))]
        + [pl.BlockSpec((SUM_ROWS, part.shape[1]), lambda i: (last, 0)) for part in small],
        [
            pl.BlockSpec((block, width), lambda i: (i, 0)),
            pl.BlockSpec((width, block), lambda i: (0, i)),
            fixed(8, width),
            fixed(1, wide),
            fixed(1, 3 * width),
        ],
        [
            shape((seq, width), BF16),
            shape((width, seq), BF16),
            shape((8, width), F32),
            shape((1, wide), F32),
            shape((1, 3 * width), F32),
        ],
    )(where, inputs, *small)


def qkv_kernel(count, slot, slots, where, a_ref, bias_ref, q, k, v, *rest):
    pieces = rest[:8]
    out_ref, kept_ref, full, sems, out_sems = rest[-5:]
    step, part = pl.program_id(0), pl.program_id(1)
    half = pieces[0].shape[2]

    def keep():
        return [
            pltpu.make_async_copy(
                full.at[:, core * half : (core + 1) * half],
                kept_ref.at[
                    :, (core * slots + slot) * 3 * PAIR : (core * slots + slot) * 3 * PAIR + half
                ],
                out_sems.at[core],
            )
            for core in range(2)
        ]

    @pl.when((step == 0) & (part == 0))
    def _():
        copies = pair_copies(where, (q, k, v), pieces, full, sems, count, slot)
        start_all(copies)
        wait_all(copies)
        start_all(keep())

    wide = out_ref.shape[1]
    column = pl.multiple_of(part * wide, wide)
    rows = (dot(a_ref[...], full[:, pl.ds(column, wide)]) + bias_ref[...]).astype(BF16)
    for begin in range(0, wide, PAIR):
        value = rows[:, begin : begin + PAIR]
        if begin // PAIR % 3 == 0:
            value = value * jnp.asarray(HEAD_DIM**-0.5, BF16)
        out_ref[:, begin : begin + PAIR] = value

    @pl.when((step == pl.num_programs(0) - 1) & (part == pl.num_programs(1) - 1))
    def _():
        wait_all(keep())


def project_qkv(where, attn_in, bias, own, pieces, count, slot, kept=()):
    seq, width = attn_in.shape
    slots = own[0].shape[1] // PAIR // 2
    half = pieces[0].shape[2]
    wide, parts, block = (2 * half, 1, 512) if slot == 0 else (half, 2, seq)
    first = 0 if slot == 0 else 1
    copies = copy_count(count) - 1 + 2 * half // PAIR
    return call(
        partial(qkv_kernel, count, slot, slots),
        "project_qkv",
        (seq // block, parts),
        [
            SCALARS,
            pl.BlockSpec((block, width), lambda i, n: (i, 0)),
            pl.BlockSpec((1, wide), lambda i, n: (0, first + n)),
        ]
        + [WHOLE] * (11 + len(kept)),
        [pl.BlockSpec((block, wide), lambda i, n: (i, first + n)), WHOLE],
        [shape((seq, 3 * width), BF16), shape((width, 3 * width), BF16)],
        [
            pltpu.VMEM((width, 2 * half), BF16),
            pltpu.SemaphoreType.DMA((copies,)),
            pltpu.SemaphoreType.DMA((2,)),
        ],
        aliases={14 + i: i for i in range(len(kept))},
    )(where, attn_in, bias, *own, *pieces, *kept)


def attend_kernel(where, lengths, places, q_ref, k_ref, v_ref, *rest):
    o_ref, e_ref, r_ref = rest[-3:]
    seq, block = k_ref.shape[0], q_ref.shape[0]
    first = lax.broadcasted_iota(jnp.int32, (seq, PAIR), 1) < HEAD_DIM
    here = lax.broadcasted_iota(jnp.int32, (block, PAIR), 1) < HEAD_DIM
    place = lax.broadcasted_iota(jnp.int32, (1, seq), 1)
    bias = jnp.where(place < lengths[places[where[3]]], 0.0, NEGATIVE).astype(F32)
    queries, keys, values = q_ref[...], k_ref[...], v_ref[...]
    zeros = jnp.zeros_like(keys)

    lanes = lax.broadcasted_iota(jnp.int32, (PAIR, PAIR), 0) < HEAD_DIM
    same = lanes == (lax.broadcasted_iota(jnp.int32, (PAIR, PAIR), 1) < HEAD_DIM)
    heads = same.astype(F32).astype(BF16)

    def longest(rows):
        return jnp.max(dot(rows * rows, heads))

    def run(shifted):
        blended, shares = [], []
        for head in range(2):
            head_keys = (
                jnp.where(first, keys, zeros) if head == 0 else jnp.where(first, zeros, keys)
            )
            scores = dot_nt(queries, head_keys) + bias
            if shifted:
                scores = scores - jnp.max(scores, axis=1, keepdims=True)
            raised = jnp.exp(scores)
            shares.append(1.0 / jnp.sum(raised, axis=1, keepdims=True))
            raised = raised.astype(BF16)
            e_ref[head] = raised
            blended.append(dot(raised, values))
        share = jnp.where(here, shares[0], shares[1])
        r_ref[...] = share
        o_ref[...] = (jnp.where(here, blended[0], blended[1]) * share).astype(BF16)

    small = longest(queries) * longest(keys) <= 3600.0

    @pl.when(small)
    def _():
        run(False)

    @pl.when(jnp.logical_not(small))
    def _():
        run(True)


def attend(cell, qkv, spots, pairs, kept=(), block=1024):
    seq, wide = qkv.shape
    total = wide // (3 * PAIR)
    there = lambda p: spots[0] + (spots[1] - spots[0]) * p
    here = lambda p: pairs[0] + (pairs[1] - pairs[0]) * p
    return call(
        attend_kernel,
        "attend",
        (2, seq // block),
        [
            SCALARS,
            SCALARS,
            SCALARS,
            pl.BlockSpec((block, PAIR), lambda p, b: (b, 3 * there(p))),
            pl.BlockSpec((seq, PAIR), lambda p, b: (0, 3 * there(p) + 1)),
            pl.BlockSpec((seq, PAIR), lambda p, b: (0, 3 * there(p) + 2)),
        ]
        + [WHOLE] * len(kept),
        [
            pl.BlockSpec((block, PAIR), lambda p, b: (b, here(p))),
            pl.BlockSpec((2, block, seq), lambda p, b: (here(p), b, 0)),
            pl.BlockSpec((block, PAIR), lambda p, b: (b, here(p))),
        ],
        [
            shape((seq, total * PAIR), BF16),
            shape((2 * total, seq, seq), BF16),
            shape((seq, total * PAIR), F32),
        ],
        aliases={6 + i: i for i in range(len(kept))},
    )(*cell, qkv, qkv, qkv, *kept)


ERF_P = 0.3275911 * 2.0**-0.5
ERF_A = (0.254829592, -0.284496736, 1.421413741, -1.453152027, 1.061405429)


def gelu_parts(values):
    bell = jnp.exp(values * values * -0.5)
    ratio = 1.0 / (1.0 + ERF_P * jnp.abs(values))
    tail = 0.5 * ERF_A[4]
    for term in ERF_A[3::-1]:
        tail = tail * ratio + 0.5 * term
    tail = tail * ratio * bell
    under = jnp.where(values > 0, 1.0 - tail, tail)
    return values * under, under + values * bell * 0.3989422804014327


def feed_kernel(
    count, where, x_ref, mix_ref, grad_ref, vec_ref, bias_ref, out_own, up_own, down_own, *rest
):
    second, third = rest[:8], rest[8:16]
    out_ref, gres_ref, gmix_ref, presum_ref, sums_ref = rest[16:21]
    halves = rest[21:27]
    w_out, w_up, w_down, t_out, t_up, t_down, sem_a, sem_b, sem_c, sem_out = rest[27:]
    step = pl.program_id(0)
    rows = up_own.shape[0] // 4
    blocks = up_own.shape[1] // 2 // second[0].shape[2]
    out_copies = column_copies(where, out_own, second, w_out, sem_a, count, blocks * rows)
    up_copies = column_copies(where, up_own, second, w_up, sem_b, count, 0)
    down_copies = row_copies(where, down_own, third, w_down, sem_c, count)

    @pl.when(step == 0)
    def _():
        start_all(out_copies)
        start_all(up_copies)
        start_all(down_copies)
        for ref in (t_out, t_up, t_down, presum_ref, sums_ref):
            ref[...] = jnp.zeros_like(ref)
        wait_all(out_copies)

    mix = mix_ref[...]
    grads = grad_ref[...]
    mixed = x_ref[...].astype(F32) + vec_ref[OUT_B : OUT_B + 1, :] + dot(mix, w_out[...])
    normed, inverse = moments(mixed)
    gain = vec_ref[GAIN_TWO : GAIN_TWO + 1, :]
    rows = (normed * gain + vec_ref[SHIFT_TWO : SHIFT_TWO + 1, :]).astype(BF16)

    @pl.when(step == 0)
    def _():
        wait_all(up_copies)
        wait_all(down_copies)

    def chunk(number, sums):
        result, grad_in = sums
        span = aligned(number * CHUNK, CHUNK, CHUNK)
        value, slope = gelu_parts(dot(rows, w_up[:, span]) + bias_ref[:, span])
        value = value.astype(BF16)
        result = result + dot(value, w_down[span, :])
        t_down[span, :] += dot_tn(value, grads)
        pre = (dot_nt(grads, w_down[span, :]) * slope).astype(BF16)
        presum_ref[:, span] += jnp.sum(pre.astype(F32), axis=0, keepdims=True)
        t_up[:, span] += dot_tn(rows, pre)
        return result, grad_in + dot_nt(pre, w_up[:, span])

    result, grad_in = lax.fori_loop(
        0,
        w_up.shape[1] // CHUNK,
        chunk,
        (mixed + vec_ref[DOWN_B : DOWN_B + 1, :], jnp.zeros(mixed.shape, F32)),
    )
    out_ref[...] = result.astype(BF16)
    grads = grads.astype(F32)
    grad_res = grads + norm_back(grad_in, normed, inverse, gain)
    gres_ref[...] = grad_res
    branch = grad_res.astype(BF16)
    gmix_ref[...] = dot_nt(branch, w_out[...]).astype(BF16)
    t_out[...] += dot_tn(mix, branch)
    sums_ref[0:1, :] += jnp.sum(grad_in * normed, axis=0, keepdims=True)
    sums_ref[1:2, :] += jnp.sum(grad_in, axis=0, keepdims=True)
    sums_ref[2:3, :] += jnp.sum(branch.astype(F32), axis=0, keepdims=True)
    sums_ref[3:4, :] += jnp.sum(grads, axis=0, keepdims=True)

    @pl.when(step == pl.num_programs(0) - 1)
    def _():
        copies = []
        half = w_down.shape[0] // 2
        part = half // count
        for place, core in enumerate((1 - where[2], where[2])):
            for z in range(count):
                begin = place * half + z * part
                source = aligned((2 * z + core) * part, part, 16)
                w_down[begin : begin + part, :] = t_down[source, :].astype(BF16)
            copies.append(
                pltpu.make_async_copy(
                    w_down.at[place * half : (place + 1) * half], halves[place], sem_out.at[place]
                )
            )
        start_all(copies)
        for number, (weight, total) in enumerate(((w_up, t_up), (w_out, t_out))):
            half = weight.shape[1] // 2
            for place, core in enumerate((1 - where[2], where[2])):
                span = slice(place * half, (place + 1) * half)
                weight[:, span] = total[:, aligned(core * half, half, 128)].astype(BF16)
                slot = 2 * number + 2 + place
                copies.append(
                    pltpu.make_async_copy(weight.at[:, span], halves[slot], sem_out.at[slot])
                )
                copies[-1].start()
        wait_all(copies)


def feed(
    where, inputs, mixed, grads, vectors, bias, out_own, up_own, down_own, second, third, count,
    block=256,
):
    seq, width = inputs.shape
    wide = up_own.shape[1]
    row = lambda n: pl.BlockSpec((block, n), lambda i: (i, 0))
    fixed = lambda a, b: pl.BlockSpec((a, b), lambda i: (0, 0))
    return call(
        partial(feed_kernel, count),
        "feed",
        (seq // block,),
        [SCALARS, row(width), row(width), row(width), fixed(*vectors.shape), fixed(1, wide)]
        + [WHOLE] * 19,
        [row(width), row(width), row(width), fixed(1, wide), fixed(8, width)] + [WHOLE] * 6,
        [
            shape((seq, width), BF16),
            shape((seq, width), F32),
            shape((seq, width), BF16),
            shape((1, wide), F32),
            shape((8, width), F32),
        ]
        + [shape((wide // 2, width), BF16)] * 2
        + [shape((width, wide // 2), BF16)] * 2
        + [shape((width, width // 2), BF16)] * 2,
        [
            pltpu.VMEM((width, width), BF16),
            pltpu.VMEM((width, wide), BF16),
            pltpu.VMEM((wide, width), BF16),
            pltpu.VMEM((width, width), F32),
            pltpu.VMEM((width, wide), F32),
            pltpu.VMEM((wide, width), F32),
        ]
        + [pltpu.SemaphoreType.DMA((2 * copy_count(count),))] * 3
        + [pltpu.SemaphoreType.DMA((6,))],
    )(where, inputs, mixed, grads, vectors, bias, out_own, up_own, down_own, *second, *third)


def attend_back_kernel(
    where, q_ref, k_ref, v_ref, do_ref, o_ref, r_ref, e_ref, in_ref, *rest
):
    out_ref, sum_ref, w_ref, k_acc, v_acc = rest[-5:]
    seq, block = k_ref.shape[0], q_ref.shape[0]
    step, last = pl.program_id(1), pl.num_programs(1) - 1
    first = lax.broadcasted_iota(jnp.int32, (seq, PAIR), 1) < HEAD_DIM
    here = lax.broadcasted_iota(jnp.int32, (block, PAIR), 1) < HEAD_DIM
    keys, values, queries = k_ref[...], v_ref[...], q_ref[...]
    zeros = jnp.zeros_like(values)

    @pl.when(step == 0)
    def _():
        k_acc[...] = jnp.zeros_like(k_acc)
        v_acc[...] = jnp.zeros_like(v_acc)

    grads = (do_ref[...].astype(F32) * r_ref[...]).astype(BF16)
    product = grads.astype(F32) * o_ref[...].astype(F32)
    whole = jnp.sum(product, axis=1, keepdims=True)
    part = jnp.sum(jnp.where(here, product, 0.0), axis=1, keepdims=True)
    inner = (part, whole - part)
    grads_t, queries_t = grads.T, queries.T
    grad_queries = []
    for head in range(2):
        head_values = (
            jnp.where(first, values, zeros) if head == 0 else jnp.where(first, zeros, values)
        )
        raised = e_ref[head]
        grad_shares = dot_nt(grads, head_values)
        grad_scores = (raised.astype(F32) * (grad_shares - inner[head])).astype(BF16)
        grad_queries.append(dot(grad_scores, keys))
        span = slice(head * HEAD_DIM, (head + 1) * HEAD_DIM)
        v_acc[span, :] += dot(grads_t[span], raised)
        k_acc[span, :] += dot(queries_t[span], grad_scores)
    rows = pl.ds(pl.multiple_of(step * block, block), block)
    mine = jnp.where(here, grad_queries[0], grad_queries[1]) * (HEAD_DIM**-0.5)
    out_ref[rows, 0:PAIR] = mine.astype(BF16)

    @pl.when(step == last)
    def _():
        out_ref[:, PAIR : 2 * PAIR] = k_acc[...].astype(BF16).T
        out_ref[:, 2 * PAIR : 3 * PAIR] = v_acc[...].astype(BF16).T
        sum_ref[...] = jnp.sum(out_ref[...].astype(F32), axis=0, keepdims=True)
        w_ref[...] = dot(in_ref[...], out_ref[...]).astype(BF16)


def attend_back(
    where, qkv, grad_mixed, mixed, shares, raised, in_t, other, block=1024
):
    seq = qkv.shape[0]
    pairs = qkv.shape[1] // (3 * PAIR) // 2

    def pair(p, w):
        return side(w, other) * pairs + p

    def there(p, w):
        return spot(p, side(w, other), pairs)

    return call(
        attend_back_kernel,
        "attend_back",
        (pairs, seq // block),
        [
            pl.BlockSpec((block, PAIR), lambda p, b, w: (b, 3 * there(p, w))),
            pl.BlockSpec((seq, PAIR), lambda p, b, w: (0, 3 * there(p, w) + 1)),
            pl.BlockSpec((seq, PAIR), lambda p, b, w: (0, 3 * there(p, w) + 2)),
            pl.BlockSpec((block, PAIR), lambda p, b, w: (b, pair(p, w))),
            pl.BlockSpec((block, PAIR), lambda p, b, w: (b, pair(p, w))),
            pl.BlockSpec((block, PAIR), lambda p, b, w: (b, pair(p, w))),
            pl.BlockSpec((2, block, seq), lambda p, b, w: (pair(p, w), b, 0)),
            pl.BlockSpec(in_t.shape, lambda p, b, w: (0, 0), pipeline_mode=pl.Buffered(1)),
        ],
        [
            pl.BlockSpec((seq, 3 * PAIR), lambda p, b, w: (0, p)),
            pl.BlockSpec((1, 3 * PAIR), lambda p, b, w: (0, p)),
            pl.BlockSpec((in_t.shape[0], 3 * PAIR), lambda p, b, w: (0, p)),
        ],
        [shape((seq, 3 * PAIR * pairs), BF16), shape((1, 3 * PAIR * pairs), F32), shape((in_t.shape[0], 3 * PAIR * pairs), BF16)],
        [pltpu.VMEM((PAIR, seq), F32)] * 2,
        prefetch=1,
    )(where, qkv, qkv, qkv, grad_mixed, mixed, shares, raised, in_t)


def input_kernel(
    where, other_ref, mine_ref, x_ref, gres_ref, vec_ref, w_other, w_mine,
    two_ref, pre_ref, sum_other, sum_mine, out_ref, sums_ref,
):
    width = x_ref.shape[1]

    @pl.when(pl.program_id(0) == 0)
    def _():
        sums_ref[...] = jnp.zeros_like(sums_ref)
        sums_ref[OUT_B : OUT_B + 1, :] = two_ref[2:3, :]
        sums_ref[GAIN_TWO : SHIFT_TWO + 1, :] = two_ref[0:2, :]
        sums_ref[DOWN_B : DOWN_B + 1, :] = two_ref[3:4, :]
        half = sum_mine.shape[1]
        for core in range(2):
            pick = jnp.where(where[2] == core, sum_mine[...], sum_other[...])
            for slot in range(half // (3 * PAIR)):
                column = (core * (half // (3 * PAIR)) + slot) * PAIR
                for row, kind in ((QUERY_B, 0), (VALUE_B, 2)):
                    begin = (3 * slot + kind) * PAIR
                    sums_ref[row : row + 1, column : column + PAIR] = pick[:, begin : begin + PAIR]
        for row in range(pre_ref.shape[1] // width):
            sums_ref[UP_B + row : UP_B + row + 1, :] = pre_ref[:, row * width : (row + 1) * width]

    grad_in = dot_nt(other_ref[...], w_other[...]) + dot_nt(mine_ref[...], w_mine[...])
    normed, inverse = moments(x_ref[...].astype(F32))
    gain = vec_ref[GAIN_ONE : GAIN_ONE + 1, :]
    out_ref[...] = (gres_ref[...] + norm_back(grad_in, normed, inverse, gain)).astype(BF16)
    sums_ref[GAIN_ONE : GAIN_ONE + 1, :] += jnp.sum(grad_in * normed, axis=0, keepdims=True)
    sums_ref[SHIFT_ONE : SHIFT_ONE + 1, :] += jnp.sum(grad_in, axis=0, keepdims=True)


def input_back(where, other, mine, inputs, grad_res, vectors, full, sums, block=256):
    seq, width = inputs.shape
    wide = other.shape[1]
    row = lambda n: pl.BlockSpec((block, n), lambda i, w: (i, 0))
    fixed = lambda a, b: pl.BlockSpec((a, b), lambda i, w: (0, 0))
    return call(
        input_kernel,
        "input_back",
        (seq // block,),
        [
            row(wide),
            row(wide),
            row(width),
            row(width),
            fixed(*vectors.shape),
            pl.BlockSpec((width, wide), lambda i, w: (0, 1 - w[2])),
            pl.BlockSpec((width, wide), lambda i, w: (0, w[2])),
        ]
        + [fixed(*part.shape) for part in sums],
        [row(width), fixed(SUM_ROWS, width)],
        [shape((seq, width), BF16), shape((SUM_ROWS, width), F32)],
        prefetch=1,
    )(where, other, mine, inputs, grad_res, vectors, full, full, *sums)


def outer_call(kernel, name, where, grid, in_specs, out_specs, out_shape, scratch, arrays):
    return call(kernel, name, grid, in_specs, out_specs, out_shape, scratch, 1)(where, *arrays)


def part_rows(where, total, outs, shards, column=0):
    rows = total.shape[0] // shards // 4
    span = slice(column, column + total.shape[1])
    for turn, out in enumerate(outs):
        for z in range(shards):
            begin = (z * 4 + (where[1] ^ turn)) * rows
            out[z, :, span] = total[aligned(begin, rows, 16), :].astype(BF16)


def side(w, other):
    return (1 - w[2]) if other else w[2]


def add_parts_kernel(shards, where, *refs):
    inputs, outs, total = refs[:-5], refs[-5:-1], refs[-1]
    begin = 0
    for mine, got in zip(inputs[0::2], inputs[1::2]):
        span = slice(begin, begin + mine.shape[1])
        total[:, span] = mine[...].astype(F32) + got[...].astype(F32)
        begin += mine.shape[1]
    part_rows(where, total, outs, shards)


def add_parts(where, pairs, count, steps=2):
    deep = pairs[0][0].shape[0]
    wide = sum(mine.shape[1] for mine, _ in pairs)
    rows = deep // count // 4
    arrays = [part for pair in pairs for part in pair]
    return outer_call(
        partial(add_parts_kernel, count // steps),
        "add_parts",
        where,
        (steps,),
        [pl.BlockSpec((deep // steps, part.shape[1]), lambda i, w: (i, 0)) for part in arrays],
        [pl.BlockSpec((count // steps, rows, wide), lambda i, w: (i, 0, 0))] * 4,
        [shape((count, rows, wide), BF16)] * 4,
        [pltpu.VMEM((deep // steps, wide), F32)],
        arrays,
    )


def total_of(refs, z):
    total = refs[0][z].astype(F32)
    for ref in refs[1:]:
        total = total + ref[z].astype(F32)
    return total.astype(BF16)


def quad_kernel(count, where, *refs):
    for step in range(count):
        refs[4 + step][...] = total_of(refs[:4], where[0] ^ step)


def quad_sum(where, parts, count):
    full = parts[0].shape
    return call(
        partial(quad_kernel, count),
        "quad_sum",
        (1,),
        [SCALARS] + [pl.BlockSpec(full, lambda i: (0, 0, 0))] * 4,
        [pl.BlockSpec(full[1:], lambda i: (0, 0))] * count,
        [shape(full[1:], BF16)] * count,
    )(where, *parts)


def quad_pairs_kernel(half, where, *refs):
    near, far = refs[4:]
    for step in range(half):
        near[step] = total_of(refs[:4], where[0] ^ (2 * step))
        far[step] = total_of(refs[:4], where[0] ^ (2 * step) ^ 1)


def quad_pairs(where, parts, count):
    full = parts[0].shape
    half = count // 2
    return call(
        partial(quad_pairs_kernel, half),
        "quad_pairs",
        (1,),
        [SCALARS] + [pl.BlockSpec(full, lambda i: (0, 0, 0))] * 4,
        [pl.BlockSpec((half, *full[1:]), lambda i: (0, 0, 0))] * 2,
        [shape((half, *full[1:]), BF16)] * 2,
    )(where, *parts)


def halve_kernel(a, b, mine, other):
    total = (a[...].astype(F32) + b[...].astype(F32)).astype(BF16)
    mine[...] = total[0]
    other[...] = total[1]


def halve(near, got):
    full = near.shape
    spec = pl.BlockSpec(full, lambda i: (0, 0, 0))
    return call(
        halve_kernel,
        "halve",
        (1,),
        [spec] * 2,
        [pl.BlockSpec(full[1:], lambda i: (0, 0))] * 2,
        [shape(full[1:], BF16)] * 2,
    )(near, got)


def blocks_of(rows, wide, width):
    return [
        (rows * number, begin, min(width, wide - begin))
        for number, begin in enumerate(range(0, wide, width))
    ]


def merge_kernel(down, down_got, two, two_got, out):
    deep, width = down.shape
    rows, wide = two.shape
    out[0:deep, :] = (down[...].astype(F32) + down_got[...].astype(F32)).astype(BF16)
    total = (two[...].astype(F32) + two_got[...].astype(F32)).astype(BF16)
    for row, begin, size in blocks_of(rows, wide, width):
        row += deep
        out[row : row + rows, 0:size] = total[:, begin : begin + size]
        if size < width:
            out[row : row + rows, size:width] = jnp.zeros((rows, width - size), BF16)


def merge(down, down_got, two, two_got):
    deep, width = down.shape
    rows, wide = two.shape
    tall = deep + rows * len(blocks_of(rows, wide, width))
    whole = lambda part: pl.BlockSpec(part.shape, lambda i: (0, 0))
    return call(
        merge_kernel,
        "merge",
        (1,),
        [whole(part) for part in (down, down_got, two, two_got)],
        pl.BlockSpec((tall, width), lambda i: (0, 0)),
        shape((tall, width), BF16),
    )(down, down_got, two, two_got)


def add_kernel(*refs):
    total = refs[0][...].astype(F32)
    for ref in refs[1:-1]:
        total = total + ref[...].astype(F32)
    refs[-1][...] = total.astype(refs[-1].dtype)


def add_all(parts):
    full = parts[0].shape
    spec = pl.BlockSpec(full, lambda i: (0,) * len(full))
    return call(
        add_kernel, "add_all", (1,), [spec] * len(parts), spec, shape(full, parts[0].dtype)
    )(*parts)


def halves_of(where, pieces, turn):
    low = where[2] == 0
    near, far = pieces[turn][...].astype(F32), pieces[4 + turn][...].astype(F32)
    return jnp.where(low, near, far), jnp.where(low, far, near)


def lay_merged_kernel(where, *refs):
    pieces, (down, out, up) = refs[:8], refs[8:]
    width, half = down.shape[1], out.shape[1] // 2
    deep = down.shape[0] // 8
    rows, wide = up.shape[0] // 4, half + up.shape[1] // 2
    for turn in range(4):
        quad = where[1] ^ turn
        for core, value in enumerate(halves_of(where, pieces, turn)):
            down[aligned((4 * core + quad) * deep, deep, 16), :] = value[0:deep]
            for row, begin, size in blocks_of(rows, wide, width):
                part = value[deep + row : deep + row + rows, 0:size]
                place = aligned(quad * rows, rows, 16)
                if begin < half:
                    out[place, core * half : (core + 1) * half] = part[:, 0:half]
                    part, begin = part[:, half:], half
                column = core * (wide - half) + begin - half
                up[place, column : column + part.shape[1]] = part


def lay_pairs_kernel(where, *refs):
    pieces, outs = refs[:8], refs[8:]
    rows, half = pieces[0].shape
    for turn in range(4):
        place = aligned((where[1] ^ turn) * rows, rows, 16)
        for core, value in enumerate(halves_of(where, pieces, turn)):
            for slot in range(half // (3 * PAIR)):
                begin = (core * (half // (3 * PAIR)) + slot) * PAIR
                for kind, out in enumerate(outs):
                    column = (3 * slot + kind) * PAIR
                    out[place, begin : begin + PAIR] = value[:, column : column + PAIR]


def lay(kernel, name, where, pieces, outs):
    spec = pl.BlockSpec(pieces[0].shape, lambda i: (0, 0))
    return call(
        kernel,
        name,
        (1,),
        [SCALARS] + [spec] * 8,
        [pl.BlockSpec(dims, lambda i: (0, 0)) for dims in outs],
        [shape(dims, F32) for dims in outs],
    )(where, *pieces)


def pick_kernel(count, where, a, b, *outs):
    total = a[...] + b[...]
    shard = outs[0].shape[0]
    for row, out in enumerate(outs[:UP_B]):
        value = total[row : row + 1, 0:shard]
        for z in range(1, count):
            value = jnp.where(where[0] == z, total[row : row + 1, z * shard : (z + 1) * shard], value)
        out[...] = value.reshape(shard)
    value = total[UP_B : UP_B + 1, :]
    for z in range(1, count):
        value = jnp.where(where[0] == z, total[UP_B + z : UP_B + z + 1, :], value)
    outs[UP_B][...] = value.reshape(outs[UP_B].shape[0])


def pick(where, a, b, shard, wide):
    sizes = [shard] * UP_B + [wide]
    return call(
        partial(pick_kernel, a.shape[1] // shard),
        "pick",
        (1,),
        [SCALARS] + [pl.BlockSpec(a.shape, lambda i: (0, 0))] * 2,
        [pl.BlockSpec((size,), lambda i: (0,)) for size in sizes],
        [shape((size,), F32) for size in sizes],
    )(where, a, b)


def tally_kernel(where, lengths, places, ids_ref, out_ref):
    ids = ids_ref[...]
    seq = ids.shape[1]
    live = lax.broadcasted_iota(jnp.int32, (1, seq), 1) < lengths[places[where[3]]]
    high, low = ids // 128, jnp.where(live, ids % 128, -1)
    tall = (lax.broadcasted_iota(jnp.int32, (TALLY_ROWS, seq), 0) == high).astype(F32).astype(BF16)
    wide = (lax.broadcasted_iota(jnp.int32, (128, seq), 0) == low).astype(F32).astype(BF16)
    out_ref[...] = dot_nt(tall, wide).astype(jnp.int32)


def tally(cell, ids):
    return call(
        tally_kernel,
        "tally",
        (1,),
        [SCALARS] * 3 + [pl.BlockSpec(ids.shape, lambda i: (0, 0))],
        pl.BlockSpec((TALLY_ROWS, 128), lambda i: (0, 0)),
        shape((TALLY_ROWS, 128), jnp.int32),
    )(*cell, ids)


def body(
    dp_size,
    fsdp_size,
    cells_in,
    out_grad,
    cell_length,
    cell_place,
    gene_ids,
    attn_norm_gain,
    attn_norm_bias,
    query_weight,
    query_bias,
    key_weight,
    value_weight,
    value_bias,
    out_weight,
    out_bias,
    ffn_norm_gain,
    ffn_norm_bias,
    up_weight,
    up_bias,
    down_weight,
    down_bias,
):
    count = fsdp_size
    seq, width = cells_in.shape[1:]
    place = lax.axis_index("dp")
    z = lax.axis_index("fsdp")
    core, quad = place & 1, (place >> 1) & 3
    where = jnp.stack([z, quad, core, place * fsdp_size + z]).astype(jnp.int32)
    cell = (where, cell_length.astype(jnp.int32), cell_place.astype(jnp.int32))

    def swap(value, mask):
        return lax.ppermute(value, "dp", [(i, i ^ mask) for i in range(dp_size)])

    def turn(value, step):
        return lax.ppermute(value, "fsdp", [(i, i ^ step) for i in range(count)])

    def from_quad(value):
        return [swap(value, 2 * mask) for mask in (1, 2, 3)]

    def to_quad(parts):
        return [swap(parts[mask], 2 * mask) for mask in (1, 2, 3)]

    def from_column(value):
        return [turn(value, step) for step in range(1, count)]

    def to_column(parts):
        return [turn(parts[step], step) for step in range(1, count)]

    def to_core(parts, beside=None, at_once=2):
        first = lambda: (
            [swap(part, 1) for part in parts[:at_once]], beside() if beside else ()
        )
        got, result = during(first)
        if at_once < len(parts):
            got = got + during(lambda: [swap(part, 1) for part in parts[at_once:]])
        return (got, result) if beside else got

    def beyond(total):
        mask = 8
        while mask < dp_size:
            total = add_all([total, swap(total, mask)])
            mask *= 2
        return total

    inputs = cells_in.reshape(seq, width)
    grads = out_grad.reshape(seq, width)
    live = cell_length[0] > 0

    def during(run):
        outs = jax.eval_shape(run)
        blank = lambda: jax.tree.map(lambda out: jnp.zeros(out.shape, out.dtype), outs)
        return lax.cond(live, run, blank)

    shard = attn_norm_gain.shape[0]
    small = [
        attn_norm_gain,
        attn_norm_bias,
        out_bias,
        ffn_norm_gain,
        ffn_norm_bias,
        down_bias,
        query_bias,
        value_bias,
        up_bias,
    ]
    own = (query_weight, key_weight, value_weight)
    pairs = width // PAIR
    deep = down_weight.shape[0] // 8
    first, rest = pack(where, *own, out_weight, up_weight, down_weight, small)

    rows, wide = first.shape[0] - SUM_ROWS, first.shape[1]
    group = 3 * PAIR

    far, counts = during(lambda: (from_column(first), tally(cell, gene_ids)))
    early, later = split(far, [(0, 0, rows, group), (0, group, rows, wide - group)])
    small = [first] + far
    last = pairs // 2

    def first_stage():
        near, norm = during(
            lambda: (
                from_quad(early),
                first_norm(where, inputs, small, shard, count * up_bias.shape[0]),
            )
        )
        near = [early] + near
        pieces = near + to_core(near, at_once=4)

        def stage():
            kept = project_qkv(where, norm[0], norm[4], own, pieces, count, 0)
            return kept, attend(cell, kept[0], (0, 1), (0, last))

        far, (kept, mixed) = during(lambda: (from_quad(later), during(stage)))
        return norm, far, kept, mixed

    rest, ((attn_in, attn_in_t, vectors, up_b, bias), far, kept, mixed) = during(
        lambda: (lax.all_gather(rest, "fsdp", axis=0), during(first_stage))
    )
    second, third = sort(where, rest, (rest.shape[1] - deep, deep))
    later = [later] + far

    def stage():
        pieces = later + to_core(later)
        out = project_qkv(where, attn_in, bias, own, pieces, count, 1, kept)
        return out, attend(cell, out[0], (2, 3), (1, 2), mixed)

    far, ((qkv, qkv_full), mixed) = during(lambda: (from_quad(second), during(stage)))
    second = [second] + far
    far, (other, (mixed, raised, shares)) = during(
        lambda: (
            from_quad(third),
            to_core(
                second,
                lambda: attend(cell, qkv, (4, 5), (last + 1, last + 2), mixed),
            ),
        )
    )
    second, third = second + other, [third] + far
    third = third + to_core(third, at_once=4)
    counts, (block_out, grad_res, grad_mixed, pre_sum, two_sums, *halves) = during(
        lambda: (
            lax.psum(counts, "fsdp"),
            feed(
                where, inputs, mixed, grads, vectors, up_b, out_weight, up_weight, down_weight,
                second, third, count,
            ),
        )
    )
    down_theirs, down_mine, up_theirs, up_mine, out_theirs, out_mine = halves

    def backward():
        down_got = during(lambda: swap(down_theirs, 1))
        down_parts = add_parts(where, [(down_mine, down_got)], count)

        got, (up_got, out_got, (grads_other, sums_other, qkv_theirs)) = during(
            lambda: (
                to_quad(down_parts),
                during(
                    lambda: (
                        swap(up_theirs, 1),
                        swap(out_theirs, 1),
                        attend_back(
                            where, qkv, grad_mixed, mixed, shares, raised, attn_in_t, True
                        ),
                    )
                ),
            )
        )
        two_parts = add_parts(where, [(out_mine, out_got), (up_mine, up_got)], count)
        down_near, down_far = quad_pairs(where, [down_parts[0]] + got, count)

        def stage():
            got, far, (grads_mine, sums_mine, mine) = during(
                lambda: (
                    swap(qkv_theirs, 1),
                    turn(down_far, 1),
                    attend_back(where, qkv, grad_mixed, mixed, shares, raised, attn_in_t, False),
                )
            )
            parts = add_parts(where, [(mine, got)], count)
            return parts, halve(down_near, far), grads_mine, sums_mine

        got, (qkv_parts, (down_piece, down_next), grads_mine, sums_mine) = during(
            lambda: (to_quad(two_parts), during(stage))
        )

        def stage():
            near, far = quad_pairs(where, [two_parts[0]] + got, count)
            far, down_got, (back, sums) = during(
                lambda: (
                    turn(far, 1),
                    turn(down_next, 2),
                    input_back(
                        where, grads_other, grads_mine, inputs, grad_res, vectors, qkv_full,
                        (two_sums, pre_sum, sums_other, sums_mine),
                    ),
                )
            )
            piece, following = halve(near, far)
            got_too, more = during(lambda: (turn(following, 2), swap(sums, 1)))
            sums = add_all([sums, more])
            merged = beyond(merge(down_piece, down_got, piece, got_too))
            return merged, back, sums

        got, (merged, input_grad, sums) = during(lambda: (to_quad(qkv_parts), during(stage)))
        qkv_parts = quad_sum(where, [qkv_parts[0]] + got, count)
        got, (side, other_side) = during(
            lambda: (to_column(qkv_parts), during(lambda: (swap(merged, 2), swap(merged, 4))))
        )
        qkv_piece = beyond(add_all([qkv_parts[0]] + got))
        far, (across, more) = during(
            lambda: (from_quad(qkv_piece), during(lambda: (swap(merged, 6), swap(sums, 2))))
        )
        qkv_pieces, merged = [qkv_piece] + far, [merged, side, other_side, across]
        sums = add_all([sums, more])
        other, more = during(lambda: ([swap(part, 1) for part in qkv_pieces], swap(sums, 4)))
        sums = sums + more
        mask = 8
        while mask < dp_size:
            sums = sums + swap(sums, mask)
            mask *= 2
        sums_got, (far, (grad_query, grad_key, grad_value)) = during(
            lambda: (
                turn(sums, 1),
                to_core(
                    merged,
                    lambda: lay(
                        lay_pairs_kernel, "lay_qkv", where, qkv_pieces + other,
                        [query_weight.shape] * 3,
                    ),
                    4,
                ),
            )
        )
        sums = add_all([sums, sums_got])
        more, (grad_down, grad_out, grad_up) = during(
            lambda: (
                turn(sums, 2),
                lay(
                    lay_merged_kernel, "lay_merged", where, merged + far,
                    [down_weight.shape, out_weight.shape, up_weight.shape],
                ),
            )
        )
        vec = pick(where, sums, more, shard, up_bias.shape[0])
        return input_grad, vec, grad_query, grad_key, grad_value, grad_out, grad_up, grad_down

    counts, results = during(lambda: (lax.psum(counts, "dp"), during(backward)))
    input_grad, vec, grad_query, grad_key, grad_value, grad_out, grad_up, grad_down = results
    gene_counts = counts.reshape(-1)[:VOCAB]

    return (
        block_out.reshape(cells_in.shape),
        input_grad.reshape(cells_in.shape),
        vec[0],
        vec[1],
        grad_query,
        vec[6],
        grad_key,
        grad_value,
        vec[7],
        grad_out,
        vec[2],
        vec[3],
        vec[4],
        grad_up,
        vec[UP_B],
        grad_down,
        vec[5],
        gene_counts,
    )


def solution(mesh):
    cells = P(("dp", "fsdp"), None, None)
    vector = P("fsdp")
    matrix = P("fsdp", None)
    in_specs = (
        cells,
        cells,
        P(),
        P(),
        P(("dp", "fsdp"), None),
        vector,
        vector,
        matrix,
        vector,
        matrix,
        matrix,
        vector,
        matrix,
        vector,
        vector,
        vector,
        matrix,
        vector,
        matrix,
        vector,
    )
    out_specs = (
        cells,
        cells,
        vector,
        vector,
        matrix,
        vector,
        matrix,
        matrix,
        vector,
        matrix,
        vector,
        vector,
        vector,
        matrix,
        vector,
        matrix,
        vector,
        P(),
    )
    return jax.shard_map(
        partial(body, mesh.shape["dp"], mesh.shape["fsdp"]),
        mesh=mesh,
        in_specs=in_specs,
        out_specs=out_specs,
        check_vma=False,
    )
```

profile of v0, /device:TPU:0, one launch (start us, length us, event | category | flops | bytes accessed | tf_op | source)
XLA Modules:
  0.0 385.0 jit_solution(6484303637416577151)
XLA Ops:
  10.6 17.7 %conditional.36 = (bf16[64,1152]{1,0:T(8,128)(2,1)}, bf16[64,1152]{1,0:T(8,128)(2,1)}, bf16[64,1152]{1,0:T(8,128)(2,1)}, s32[288,128]{1,0:T(8,128)S(1)}) conditional(s32[]{:T(128)} %convert_element_type.52, () %tuple.307, (bf16[64,1152]{1,0:T(8,128)(2,1)S(1)}, s32[4]{0:T(128)S(1)}, s32[32]{0:T(128)S(1)}, s32[32]{0:T(128)S(1)}, ...), branch_computations={%region_0.0_spmd, %region_1.0_spmd} | conditional | flops 1024 | bytes 1770648 | solution.py:1087
  29.6 39.0 %conditional.37 = (bf16[4,240,768]{2,1,0:T(8,128)(2,1)}, bf16[1024,768]{1,0:T(8,128)(2,1)}, bf16[768,1024]{1,0:T(8,128)(2,1)}, f32[8,768]{1,0:T(8,128)}, f32[1,3...) conditional(s32[]{:T(128)} %convert_element_type.52, () %tuple.310, ...), branch_computations={%region_2.0_spmd, %region_3.0_spmd} | conditional | flops 3075 | bytes 51620072 | solution.py:1087
  30.3 29.7 %conditional.4 = (bf16[1024,768]{1,0:T(8,128)(2,1)}, bf16[768,1024]{1,0:T(8,128)(2,1)}, f32[8,768]{1,0:T(8,128)}, f32[1,3072]{1,0:T(1,128)}, f32[1,2304]{1,0:T(1...) conditional(s32[]{:T(128)} %convert_element_type.21, () %tuple.185, ...), branch_computations={%region_4.0_spmd, %region_5.0_spmd} | conditional | flops 3074 | bytes 46090204 | solution.py:1087
  40.6 18.4 %conditional.3 = (bf16[3,48,768]{2,1,0:T(8,128)(2,1)}, bf16[3,48,768]{2,1,0:T(8,128)(2,1)}, bf16[3,48,768]{2,1,0:T(8,128)(2,1)}, bf16[1024,2304]{1,0:T(8,128)(2,...) conditional(s32[]{:T(128)} %convert_element_type.15, () %tuple.180, ...), branch_computations={%region_10.0_spmd, %region_11.0_spmd} | conditional | flops 2049 | bytes 40796528 | solution.py:1087
  44.1 14.7 %conditional = (bf16[1024,2304]{1,0:T(8,128)(2,1)}, bf16[768,2304]{1,0:T(8,128)(2,1)}, bf16[1024,768]{1,0:T(8,128)(2,1)}, bf16[12,1024,1024]{2,1,0:T(8,128)(2,1)}, f32[1024,768]{1,0:T(8,128)}) conditional(s32[]{:T(128)} %convert_element_type.14, () %tuple.175, (s32[4]{0:T(128)S(1)}, bf16[1024,768]{1,0:T(8,128)(2,1)}, f32[1,2304]{1,0:T(1,128)}, ...), branch_computations={%region_12.0_spmd, %region_13.0_spmd} | conditional | flops 2048 | bytes 38142004 | solution.py:1087
  70.8 31.4 %conditional.38 = (bf16[3,144,768]{2,1,0:T(8,128)(2,1)}, bf16[3,144,768]{2,1,0:T(8,128)(2,1)}, bf16[3,144,768]{2,1,0:T(8,128)(2,1)}, bf16[1024,2304]{1,0:T(8,128...) conditional(s32[]{:T(128)} %convert_element_type.52, () %tuple.312, ...), branch_computations={%region_14.0_spmd, %region_15.0_spmd} | conditional | flops 2050 | bytes 46104960 | solution.py:1087
  74.3 21.1 %conditional.7 = (bf16[1024,2304]{1,0:T(8,128)(2,1)}, bf16[768,2304]{1,0:T(8,128)(2,1)}, bf16[1024,768]{1,0:T(8,128)(2,1)}, bf16[12,1024,1024]{2,1,0:T(8,128)(2,1)}, f32[1024,768]{1,0:T(8,128)}) conditional(s32[]{:T(128)} %convert_element_type.27, () %tuple.199, (pred[]{:T(512)}, bf16[3,48,768]{2,1,0:T(8,128)(2,1)S(1)}, ...), branch_computations={%region_16.0_spmd, %region_17.0_spmd} | conditional | flops 2049 | bytes 38142004 | solution.py:1087
  102.2 36.8 %conditional.39 = (bf16[3,96,768]{2,1,0:T(8,128)(2,1)}, bf16[3,96,768]{2,1,0:T(8,128)(2,1)}, bf16[3,96,768]{2,1,0:T(8,128)(2,1)}, bf16[3,144,768]{2,1,0:T(8,128)...) conditional(s32[]{:T(128)} %convert_element_type.52, () %tuple.309, ...), branch_computations={%region_22.0_spmd, %region_23.0_spmd} | conditional | flops 1025 | bytes 41828792 | solution.py:1087
  143.0 61.0 %conditional.41 = (s32[288,128]{1,0:T(8,128)}, f32[1024,768]{1,0:T(8,128)}, bf16[1024,768]{1,0:T(8,128)(2,1)S(1)}, f32[1,3072]{1,0:T(1,128)S(1)}, f32[8,768]{1,0...) conditional(s32[]{:T(128)} %convert_element_type.52, () %tuple.306, ...), branch_computations={%region_30.0_spmd, %region_31.0_spmd} | conditional | flops 37888 | bytes 17092736 | solution.py:1087
  143.9 59.7 %feed.1 = (bf16[1024,768]{1,0:T(8,128)(2,1)}, f32[1024,768]{1,0:T(8,128)}, bf16[1024,768]{1,0:T(8,128)(2,1)S(1)}, f32[1,3072]{1,0:T(1,128)S(1)}, f32[8,768]{1,0:...) custom-call(s32[4]{0:T(128)S(1)} %get-tuple-element.991.where, ...), custom_call_target="tpu_custom_call" | custom-call | flops 1024 | bytes 1024 | tf_op jit(solution)/shard_map/cond/branch_1_fun/feed/pallas_call | solution.py:591
  204.0 172.5 %conditional.42 = (f32[192]{0:T(256)}, f32[192]{0:T(256)}, f32[192]{0:T(256)}, f32[192]{0:T(256)}, f32[192]{0:T(256)}, /*index=5*/f32[192]{0:T(256)}, f32[192]{0...) conditional(s32[]{:T(128)} %convert_element_type.52, () %tuple.318, ...), branch_computations={%region_33.0_spmd, %region_34.0_spmd} | conditional | flops 68618 | bytes 75543472 | solution.py:1087
  204.8 170.6 %conditional.28 = (f32[192]{0:T(256)}, f32[192]{0:T(256)}, f32[192]{0:T(256)}, f32[192]{0:T(256)}, f32[192]{0:T(256)}, /*index=5*/f32[192]{0:T(256)}, f32[192]{0...) conditional(s32[]{:T(128)} %convert_element_type.50, () %tuple.287, ...), branch_computations={%region_35.0_spmd, %region_36.72_spmd} | conditional | flops 31753 | bytes 74658392 | solution.py:1087
  214.1 30.0 %conditional.20 = (bf16[4,96,768]{2,1,0:T(8,128)(2,1)}, bf16[4,96,768]{2,1,0:T(8,128)(2,1)}, bf16[4,96,768]{2,1,0:T(8,128)(2,1)}, bf16[768,1536]{1,0:T(8,128)(2,...) conditional(s32[]{:T(128)} %convert_element_type.48, () %tuple.271, ...), branch_computations={%region_39.0_spmd, %region_40.41_spmd} | conditional | flops 1025 | bytes 18875772 | solution.py:1087
  217.6 19.9 %conditional.10 = (bf16[768,1536]{1,0:T(8,128)(2,1)}, bf16[768,384]{1,0:T(8,128)(2,1)}, bf16[1024,1152]{1,0:T(8,128)(2,1)}, f32[1,1152]{1,0:T(1,128)}, bf16[768,1152]{1,0:T(8,128)(2,1)}) conditional(s32[]{:T(128)} %convert_element_type.34, () %tuple.221, (bf16[768,1536]{1,0:T(8,128)(2,1)}, bf16[768,384]{1,0:T(8,128)(2,1)}, s32[4]{0:T(128)S(1)}, ...), branch_computations={%region_41.39_spmd, %region_42.0_spmd} | conditional | flops 1024 | bytes 11797624 | solution.py:1087
  218.1 19.4 %attend_back.2 = (bf16[1024,1152]{1,0:T(8,128)(2,1)}, f32[1,1152]{1,0:T(1,128)}, bf16[768,1152]{1,0:T(8,128)(2,1)}) custom-call(s32[4]{0:T(128)S(1)} %get-tuple-element.1029.where, bf16[1024,2304]{1,0:T(8,128)(2,1)} %get-tuple-element.1030.q_ref.k_ref.v_ref, bf16[1024,2304]{1,0:T(8,128)(2,1)} %get-tuple-element.1030.q_ref.k_ref.v_ref, ...), custom_call_target="tpu_custom_call" | custom-call | flops 1024 | bytes 1024 | tf_op jit(solution)/shard_map/cond/branch_1_fun/cond/branch_1_fun/cond/branch_1_fun/cond/branch_1_fun/attend_back/pallas_call | solution.py:679
  251.5 35.7 %conditional.21 = (bf16[4,48,1920]{2,1,0:T(8,128)(2,1)}, bf16[4,48,1920]{2,1,0:T(8,128)(2,1)}, bf16[4,48,1920]{2,1,0:T(8,128)(2,1)}, bf16[4,48,1152]{2,1,0:T(8,1...) conditional(s32[]{:T(128)} %convert_element_type.48, () %tuple.270, ...), branch_computations={%region_43.42_spmd, %region_44.47_spmd} | conditional | flops 3074 | bytes 17108530 | solution.py:1087
  255.0 26.4 %conditional.12 = (bf16[4,48,1152]{2,1,0:T(8,128)(2,1)}, bf16[4,48,1152]{2,1,0:T(8,128)(2,1)}, bf16[4,48,1152]{2,1,0:T(8,128)(2,1)}, bf16[4,48,1152]{2,1,0:T(8,1...) conditional(s32[]{:T(128)} %convert_element_type.38, () %tuple.231, ...), branch_computations={%region_45.43_spmd, %region_46.46_spmd} | conditional | flops 3073 | bytes 8260869 | solution.py:1087
  255.0 20.8 %conditional.11 = (bf16[768,1152]{1,0:T(8,128)(2,1)}, bf16[2,96,768]{2,1,0:T(8,128)(2,1)}, bf16[1024,1152]{1,0:T(8,128)(2,1)}, f32[1,1152]{1,0:T(1,128)}, bf16[768,1152]{1,0:T(8,128)(2,1)}) conditional(s32[]{:T(128)} %convert_element_type.37, () %tuple.228, (bf16[768,1152]{1,0:T(8,128)(2,1)}, bf16[2,96,768]{2,1,0:T(8,128)(2,1)}, s32[4]{0:T(128)S(1)}, ...), branch_computations={%region_47.44_spmd, %region_48.0_spmd} | conditional | flops 1024 | bytes 8258680 | solution.py:1087
  256.4 19.3 %attend_back.3 = (bf16[1024,1152]{1,0:T(8,128)(2,1)}, f32[1,1152]{1,0:T(1,128)}, bf16[768,1152]{1,0:T(8,128)(2,1)}) custom-call(s32[4]{0:T(128)S(1)} %get-tuple-element.1059.where, bf16[1024,2304]{1,0:T(8,128)(2,1)} %get-tuple-element.1060.q_ref.k_ref.v_ref, bf16[1024,2304]{1,0:T(8,128)(2,1)} %get-tuple-element.1060.q_ref.k_ref.v_ref, ...), custom_call_target="tpu_custom_call" | custom-call | flops 1024 | bytes 1024 | tf_op jit(solution)/shard_map/cond/branch_1_fun/cond/branch_1_fun/cond/branch_1_fun/cond/branch_1_fun/cond/branch_1_fun/attend_back/pallas_call | solution.py:679
  287.2 35.0 %conditional.22 = (bf16[4,48,1152]{2,1,0:T(8,128)(2,1)}, bf16[4,48,1152]{2,1,0:T(8,128)(2,1)}, bf16[4,48,1152]{2,1,0:T(8,128)(2,1)}, bf16[240,768]{1,0:T(8,128)(...) conditional(s32[]{:T(128)} %convert_element_type.48, () %tuple.269, (bf16[4,48,1152]{2,1,0:T(8,128)(2,1)}, ...), branch_computations={%region_49.48_spmd, %region_50.55_spmd} | conditional | flops 5122 | bytes 8385116 | solution.py:1087
  290.8 31.4 %conditional.15 = (bf16[240,768]{1,0:T(8,128)(2,1)}, f32[16,768]{1,0:T(8,128)}, bf16[1,1024,768]{2,1,0:T(8,128)(2,1)}) conditional(s32[]{:T(128)} %convert_element_type.40, () %tuple.245, (pred[]{:T(512)}, s32[4]{0:T(128)S(1)}, bf16[4,48,1920]{2,1,0:T(8,128)(2,1)}, bf16[4,48,1920]{2,1,0:T(8,128)(2,1)}, bf16[4,48,1920]{2,1,0:T(8,128)(2,1)}, ...), branch_computations={%region_51.49_spmd, %region_52.54_spmd} | conditional | flops 5121 | bytes 3076383 | solution.py:1087
  293.5 13.2 %conditional.13 = (bf16[2,48,1920]{2,1,0:T(8,128)(2,1)}, bf16[96,768]{1,0:T(8,128)(2,1)}, f32[16,768]{1,0:T(8,128)S(1)}, bf16[1,1024,768]{2,1,0:T(8,128)(2,1)}) conditional(s32[]{:T(128)} %convert_element_type.39, () %tuple.240, (bf16[2,48,1920]{2,1,0:T(8,128)(2,1)S(1)}, bf16[96,768]{1,0:T(8,128)(2,1)}, s32[4]{0:T(128)S(1)}, ...), branch_computations={%region_53.50_spmd, %region_54.0_spmd} | conditional | flops 1024 | bytes 2138154 | solution.py:1087
  324.3 13.6 %conditional.23 = (bf16[48,1152]{1,0:T(8,128)(2,1)}, bf16[48,1152]{1,0:T(8,128)(2,1)}, bf16[48,1152]{1,0:T(8,128)(2,1)}, bf16[240,768]{1,0:T(8,128)(2,1)}, bf16[240,768]{1,0:T(8,128)(2,1)}) conditional(s32[]{:T(128)} %convert_element_type.48, () %tuple.277, (bf16[48,1152]{1,0:T(8,128)(2,1)S(1)}, bf16[48,1152]{1,0:T(8,128)(2,1)S(1)}, ...), branch_computations={%region_57.56_spmd, %region_58.59_spmd} | conditional | flops 1 | bytes 4276485 | solution.py:1087
  339.0 15.3 %conditional.24 = (bf16[48,1152]{1,0:T(8,128)(2,1)}, bf16[48,1152]{1,0:T(8,128)(2,1)}, bf16[48,1152]{1,0:T(8,128)(2,1)}, bf16[240,768]{1,0:T(8,128)(2,1)}, f32[16,768]{1,0:T(8,128)}) conditional(s32[]{:T(128)} %convert_element_type.48, () %tuple.276, (bf16[48,1152]{1,0:T(8,128)(2,1)S(1)}, pred[]{:T(512)}, bf16[240,768]{1,0:T(8,128)(2,1)}, ...), branch_computations={%region_61.60_spmd, %region_62.63_spmd} | conditional | flops 1 | bytes 2998549 | solution.py:1087
  (214 shorter events, 340.7 us)
Async XLA Ops:
  29.6 38.7 %all-gather.3.cloned.1.call-start = ((), (), s32[]{:S(2)}) async-start(), calls=%async_computation | async-start | bytes 1843200 | tf_op jit(solution)/shard_map/cond/branch_1_fun/all_gather | solution.py:1132
  40.6 18.2 %collective-permute-start.12 = (bf16[3,48,768]{2,1,0:T(8,128)(2,1)S(1)}, bf16[3,48,768]{2,1,0:T(8,128)(2,1)}, u32[]{:S(2)}, u32[]{:S(2)}) collective-permute-start(bf16[3,48,768]{2,1,0:T(8,128)(2,1)S(1)} %get-tuple-element.812), channel_id=1, source_target_pairs={{0,24},{4,28},{8,16},{12,20},{16,8},{20,12},{24,0},{28,4},{1,25},{... | collective-permute-start | bytes 663560 | tf_op jit(solution)/shard_map/cond/branch_1_fun/cond/branch_1_fun/cond/branch_1_fun/ppermute | solution.py:1047
  42.2 16.6 %collective-permute-start.11 = (bf16[3,48,768]{2,1,0:T(8,128)(2,1)S(1)}, bf16[3,48,768]{2,1,0:T(8,128)(2,1)}, u32[]{:S(2)}, u32[]{:S(2)}) collective-permute-start(bf16[3,48,768]{2,1,0:T(8,128)(2,1)S(1)} %get-tuple-element.812), channel_id=1, source_target_pairs={{0,16},{4,20},{8,24},{12,28},{16,0},{20,4},{24,8},{28,12},{1,17},{... | collective-permute-start | bytes 663560 | tf_op jit(solution)/shard_map/cond/branch_1_fun/cond/branch_1_fun/cond/branch_1_fun/ppermute | solution.py:1047
  70.8 24.6 %collective-permute-start.19 = (bf16[3,144,768]{2,1,0:T(8,128)(2,1)S(1)}, bf16[3,144,768]{2,1,0:T(8,128)(2,1)}, u32[]{:S(2)}, u32[]{:S(2)}) collective-permute-start(bf16[3,144,768]{2,1,0:T(8,128)(2,1)S(1)} %get-tuple-element.928), channel_id=1, source_target_pairs={{0,24},{4,28},{8,16},{12,20},{16,8},{20,12},{24,0},{28,4},{1,25},{... | collective-permute-start | bytes 1990664 | tf_op jit(solution)/shard_map/cond/branch_1_fun/ppermute | solution.py:1047
  73.2 28.9 %collective-permute-start.18 = (bf16[3,144,768]{2,1,0:T(8,128)(2,1)S(1)}, bf16[3,144,768]{2,1,0:T(8,128)(2,1)}, u32[]{:S(2)}, u32[]{:S(2)}) collective-permute-start(bf16[3,144,768]{2,1,0:T(8,128)(2,1)S(1)} %get-tuple-element.928), channel_id=1, source_target_pairs={{0,16},{4,20},{8,24},{12,28},{16,0},{20,4},{24,8},{28,12},{1,17},{... | collective-permute-start | bytes 1990664 | tf_op jit(solution)/shard_map/cond/branch_1_fun/ppermute | solution.py:1047
  73.8 28.5 %collective-permute-start.17 = (bf16[3,144,768]{2,1,0:T(8,128)(2,1)S(1)}, bf16[3,144,768]{2,1,0:T(8,128)(2,1)}, u32[]{:S(2)}, u32[]{:S(2)}) collective-permute-start(bf16[3,144,768]{2,1,0:T(8,128)(2,1)S(1)} %get-tuple-element.928), channel_id=1, source_target_pairs={{0,8},{4,12},{8,0},{12,4},{16,24},{20,28},{24,16},{28,20},{1,9},{5... | collective-permute-start | bytes 1990664 | tf_op jit(solution)/shard_map/cond/branch_1_fun/ppermute | solution.py:1047
  116.1 16.8 %collective-permute-start.26 = (bf16[3,96,768]{2,1,0:T(8,128)(2,1)}, bf16[3,96,768]{2,1,0:T(8,128)(2,1)}, u32[]{:S(2)}, u32[]{:S(2)}) collective-permute-start(bf16[3,96,768]{2,1,0:T(8,128)(2,1)} %get-tuple-element.966), channel_id=1, source_target_pairs={{0,24},{4,28},{8,16},{12,20},{16,8},{20,12},{24,0},{28,4},{1,25},{... | collective-permute-start | bytes 1327112 | tf_op jit(solution)/shard_map/cond/branch_1_fun/ppermute | solution.py:1047
  117.9 21.0 %collective-permute-start.25 = (bf16[3,96,768]{2,1,0:T(8,128)(2,1)}, bf16[3,96,768]{2,1,0:T(8,128)(2,1)}, u32[]{:S(2)}, u32[]{:S(2)}) collective-permute-start(bf16[3,96,768]{2,1,0:T(8,128)(2,1)} %get-tuple-element.966), channel_id=1, source_target_pairs={{0,16},{4,20},{8,24},{12,28},{16,0},{20,4},{24,8},{28,12},{1,17},{... | collective-permute-start | bytes 1327112 | tf_op jit(solution)/shard_map/cond/branch_1_fun/ppermute | solution.py:1047
  118.9 20.1 %collective-permute-start.24 = (bf16[3,96,768]{2,1,0:T(8,128)(2,1)}, bf16[3,96,768]{2,1,0:T(8,128)(2,1)}, u32[]{:S(2)}, u32[]{:S(2)}) collective-permute-start(bf16[3,96,768]{2,1,0:T(8,128)(2,1)} %get-tuple-element.966), channel_id=1, source_target_pairs={{0,8},{4,12},{8,0},{12,4},{16,24},{20,28},{24,16},{28,20},{1,9},{5... | collective-permute-start | bytes 1327112 | tf_op jit(solution)/shard_map/cond/branch_1_fun/ppermute | solution.py:1047
  143.0 60.6 %all-reduce.3.cloned.1.call-start = ((), (), s32[]{:S(2)}) async-start(), calls=%async_computation.1 | async-start | bytes 294912 | tf_op jit(solution)/shard_map/cond/branch_1_fun/psum | solution.py:1157
  204.0 171.4 %all-reduce.5.cloned.1.call-start = ((), (), s32[]{:S(2)}) async-start(), calls=%async_computation.2 | async-start | bytes 294912 | tf_op jit(solution)/shard_map/cond/branch_1_fun/psum | solution.py:1263
  214.1 23.4 %collective-permute-start.34 = (bf16[4,96,768]{2,1,0:T(8,128)(2,1)}, bf16[4,96,768]{2,1,0:T(8,128)(2,1)}, u32[]{:S(2)}, u32[]{:S(2)}) collective-permute-start(bf16[4,96,768]{2,1,0:T(8,128)(2,1)} %get-tuple-element.1039), channel_id=1, source_target_pairs={{0,8},{4,12},{8,0},{12,4},{16,24},{20,28},{24,16},{28,20},{1,9},{5... | collective-permute-start | bytes 1769480 | tf_op jit(solution)/shard_map/cond/branch_1_fun/cond/branch_1_fun/cond/branch_1_fun/ppermute | solution.py:1047
  215.2 28.8 %collective-permute-start.35 = (bf16[4,96,768]{2,1,0:T(8,128)(2,1)}, bf16[4,96,768]{2,1,0:T(8,128)(2,1)}, u32[]{:S(2)}, u32[]{:S(2)}) collective-permute-start(bf16[4,96,768]{2,1,0:T(8,128)(2,1)} %get-tuple-element.1040), channel_id=1, source_target_pairs={{0,16},{4,20},{8,24},{12,28},{16,0},{20,4},{24,8},{28,12},{1,17},{... | collective-permute-start | bytes 1769480 | tf_op jit(solution)/shard_map/cond/branch_1_fun/cond/branch_1_fun/cond/branch_1_fun/ppermute | solution.py:1047
  215.8 28.2 %collective-permute-start.36 = (bf16[4,96,768]{2,1,0:T(8,128)(2,1)}, bf16[4,96,768]{2,1,0:T(8,128)(2,1)}, u32[]{:S(2)}, u32[]{:S(2)}) collective-permute-start(bf16[4,96,768]{2,1,0:T(8,128)(2,1)} %get-tuple-element.1041), channel_id=1, source_target_pairs={{0,24},{4,28},{8,16},{12,20},{16,8},{20,12},{24,0},{28,4},{1,25},{... | collective-permute-start | bytes 1769480 | tf_op jit(solution)/shard_map/cond/branch_1_fun/cond/branch_1_fun/cond/branch_1_fun/ppermute | solution.py:1047
  217.6 19.9 %collective-permute-start.32 = (bf16[768,1536]{1,0:T(8,128)(2,1)}, bf16[768,1536]{1,0:T(8,128)(2,1)}, u32[]{:S(2)}, u32[]{:S(2)}) collective-permute-start(bf16[768,1536]{1,0:T(8,128)(2,1)} %get-tuple-element.1027), channel_id=1, source_target_pairs={{0,4},{4,0},{8,12},{12,8},{16,20},{20,16},{24,28},{28,24},{1,5},{5... | collective-permute-start | bytes 7077896 | tf_op jit(solution)/shard_map/cond/branch_1_fun/cond/branch_1_fun/cond/branch_1_fun/cond/branch_1_fun/ppermute | solution.py:1047
  217.6 19.9 %collective-permute-start.33 = (bf16[768,384]{1,0:T(8,128)(2,1)}, bf16[768,384]{1,0:T(8,128)(2,1)}, u32[]{:S(2)}, u32[]{:S(2)}) collective-permute-start(bf16[768,384]{1,0:T(8,128)(2,1)} %get-tuple-element.1028), channel_id=1, source_target_pairs={{0,4},{4,0},{8,12},{12,8},{16,20},{20,16},{24,28},{28,24},{1,5},{5... | collective-permute-start | bytes 1769480 | tf_op jit(solution)/shard_map/cond/branch_1_fun/cond/branch_1_fun/cond/branch_1_fun/cond/branch_1_fun/ppermute | solution.py:1047
  251.5 29.9 %collective-permute-start.39 = (bf16[4,48,1920]{2,1,0:T(8,128)(2,1)}, bf16[4,48,1920]{2,1,0:T(8,128)(2,1)}, u32[]{:S(2)}, u32[]{:S(2)}) collective-permute-start(bf16[4,48,1920]{2,1,0:T(8,128)(2,1)} %get-tuple-element.1091), channel_id=1, source_target_pairs={{0,8},{4,12},{8,0},{12,4},{16,24},{20,28},{24,16},{28,20},{1,9},{5... | collective-permute-start | bytes 2211848 | tf_op jit(solution)/shard_map/cond/branch_1_fun/cond/branch_1_fun/cond/branch_1_fun/ppermute | solution.py:1047
  252.1 29.4 %collective-permute-start.40 = (bf16[4,48,1920]{2,1,0:T(8,128)(2,1)}, bf16[4,48,1920]{2,1,0:T(8,128)(2,1)}, u32[]{:S(2)}, u32[]{:S(2)}) collective-permute-start(bf16[4,48,1920]{2,1,0:T(8,128)(2,1)} %get-tuple-element.1092), channel_id=1, source_target_pairs={{0,16},{4,20},{8,24},{12,28},{16,0},{20,4},{24,8},{28,12},{1,17},{... | collective-permute-start | bytes 2211848 | tf_op jit(solution)/shard_map/cond/branch_1_fun/cond/branch_1_fun/cond/branch_1_fun/ppermute | solution.py:1047
  253.6 32.7 %collective-permute-start.41 = (bf16[4,48,1920]{2,1,0:T(8,128)(2,1)}, bf16[4,48,1920]{2,1,0:T(8,128)(2,1)}, u32[]{:S(2)}, u32[]{:S(2)}) collective-permute-start(bf16[4,48,1920]{2,1,0:T(8,128)(2,1)} %get-tuple-element.1093), channel_id=1, source_target_pairs={{0,24},{4,28},{8,16},{12,20},{16,8},{20,12},{24,0},{28,4},{1,25},{... | collective-permute-start | bytes 2211848 | tf_op jit(solution)/shard_map/cond/branch_1_fun/cond/branch_1_fun/cond/branch_1_fun/ppermute | solution.py:1047
  255.1 20.6 %collective-permute-start.37 = (bf16[768,1152]{1,0:T(8,128)(2,1)}, bf16[768,1152]{1,0:T(8,128)(2,1)}, u32[]{:S(2)}, u32[]{:S(2)}) collective-permute-start(bf16[768,1152]{1,0:T(8,128)(2,1)} %get-tuple-element.1057), channel_id=1, source_target_pairs={{0,4},{4,0},{8,12},{12,8},{16,20},{20,16},{24,28},{28,24},{1,5},{5... | collective-permute-start | bytes 5308424 | tf_op jit(solution)/shard_map/cond/branch_1_fun/cond/branch_1_fun/cond/branch_1_fun/cond/branch_1_fun/cond/branch_1_fun/ppermute | solution.py:1047
  255.2 20.5 %collective-permute-start.38 = (bf16[2,96,768]{2,1,0:T(8,128)(2,1)}, bf16[2,96,768]{2,1,0:T(8,128)(2,1)}, u32[]{:S(2)}, u32[]{:S(2)}) collective-permute-start(bf16[2,96,768]{2,1,0:T(8,128)(2,1)} %get-tuple-element.1058), channel_id=1, source_target_pairs={{0,1},{1,0},{2,3},{3,2},{4,5},{5,4},{6,7},{7,6},{8,9},{9,8},{10,11... | collective-permute-start | bytes 884744 | tf_op jit(solution)/shard_map/cond/branch_1_fun/cond/branch_1_fun/cond/branch_1_fun/cond/branch_1_fun/cond/branch_1_fun/ppermute | solution.py:1050
  287.2 34.9 %collective-permute-start.46 = (bf16[4,48,1152]{2,1,0:T(8,128)(2,1)}, bf16[4,48,1152]{2,1,0:T(8,128)(2,1)}, u32[]{:S(2)}, u32[]{:S(2)}) collective-permute-start(bf16[4,48,1152]{2,1,0:T(8,128)(2,1)} %get-tuple-element.1158), channel_id=1, source_target_pairs={{0,8},{4,12},{8,0},{12,4},{16,24},{20,28},{24,16},{28,20},{1,9},{5... | collective-permute-start | bytes 1327112 | tf_op jit(solution)/shard_map/cond/branch_1_fun/cond/branch_1_fun/cond/branch_1_fun/ppermute | solution.py:1047
  288.0 34.2 %collective-permute-start.47 = (bf16[4,48,1152]{2,1,0:T(8,128)(2,1)}, bf16[4,48,1152]{2,1,0:T(8,128)(2,1)}, u32[]{:S(2)}, u32[]{:S(2)}) collective-permute-start(bf16[4,48,1152]{2,1,0:T(8,128)(2,1)} %get-tuple-element.1159), channel_id=1, source_target_pairs={{0,16},{4,20},{8,24},{12,28},{16,0},{20,4},{24,8},{28,12},{1,17},{... | collective-permute-start | bytes 1327112 | tf_op jit(solution)/shard_map/cond/branch_1_fun/cond/branch_1_fun/cond/branch_1_fun/ppermute | solution.py:1047
  289.2 33.0 %collective-permute-start.48 = (bf16[4,48,1152]{2,1,0:T(8,128)(2,1)}, bf16[4,48,1152]{2,1,0:T(8,128)(2,1)}, u32[]{:S(2)}, u32[]{:S(2)}) collective-permute-start(bf16[4,48,1152]{2,1,0:T(8,128)(2,1)} %get-tuple-element.1160), channel_id=1, source_target_pairs={{0,24},{4,28},{8,16},{12,20},{16,8},{20,12},{24,0},{28,4},{1,25},{... | collective-permute-start | bytes 1327112 | tf_op jit(solution)/shard_map/cond/branch_1_fun/cond/branch_1_fun/cond/branch_1_fun/ppermute | solution.py:1047
  (59 other events, 465.8 us)
Sparse Core Ops, SparseCore 0:
  32.6 35.6 all-gather.2
  146.8 33.5 all-reduce.2
  208.3 64.0 all-reduce.4
where the time goes:
time: 385 us
  Pallas kernels  198 us (51%)
  waiting for transfers between devices  90.1 us (23%)
  starting transfers between devices  59.8 us (16%)
  loops' own time  19.2 us (5%)
  between operations  14.9 us (4%)
    ppermute x58, waiting for transfers between devices, swap(): return lax.ppermute(value, 'dp', [(i, i ^ mask) for i in range(dp_size)])  61 us
    pallas_call x1, Pallas kernels, feed(): call(partial(feed_kernel, count), 'feed', (seq // block,), [SCALARS, row(...  59.7 us
    ppermute x58, starting transfers between devices, swap(): return lax.ppermute(value, 'dp', [(i, i ^ mask) for i in range(dp_size)])  41.2 us
    pallas_call x2, Pallas kernels, attend_back(): call(attend_back_kernel, 'attend_back', (pairs, seq // block), [pl.BlockS...  38.7 us
    pallas_call x3, Pallas kernels, attend(): call(attend_kernel, 'attend', (2, seq // block), [SCALARS, SCALARS, SCALA...  28.1 us
    another operation x36, loops' own time, during(): return lax.cond(live, run, blank)  19.2 us
    ppermute x12, waiting for transfers between devices, turn(): return lax.ppermute(value, 'fsdp', [(i, i ^ step) for i in range(count)])  18.8 us
    ppermute x12, starting transfers between devices, turn(): return lax.ppermute(value, 'fsdp', [(i, i ^ step) for i in range(count)])  18.6 us
  transfers between devices with their start and end apart: 73, of which 32 were waited for; matrix products, arithmetic and copies ran while one was open for 0% of the time, Pallas kernels for 50%

commit v1 on v0

--- a/solution.py
+++ b/solution.py
@@ -397,7 +397,6 @@
     o_ref, e_ref, r_ref = rest[-3:]
     seq, block = k_ref.shape[0], q_ref.shape[0]
     first = lax.broadcasted_iota(jnp.int32, (seq, PAIR), 1) < HEAD_DIM
-    here = lax.broadcasted_iota(jnp.int32, (block, PAIR), 1) < HEAD_DIM
     place = lax.broadcasted_iota(jnp.int32, (1, seq), 1)
     bias = jnp.where(place < lengths[places[where[3]]], 0.0, NEGATIVE).astype(F32)
     queries, keys, values = q_ref[...], k_ref[...], v_ref[...]
@@ -410,33 +409,39 @@
     def longest(rows):
         return jnp.max(dot(rows * rows, heads))
 
-    def run(shifted):
+    def run(rows, size, shifted):
+        here = lax.broadcasted_iota(jnp.int32, (size, PAIR), 1) < HEAD_DIM
+        part = q_ref[rows, :]
         blended, shares = [], []
         for head in range(2):
             head_keys = (
                 jnp.where(first, keys, zeros) if head == 0 else jnp.where(first, zeros, keys)
             )
-            scores = dot_nt(queries, head_keys) + bias
+            scores = dot_nt(part, head_keys) + bias
             if shifted:
                 scores = scores - jnp.max(scores, axis=1, keepdims=True)
             raised = jnp.exp(scores)
             shares.append(1.0 / jnp.sum(raised, axis=1, keepdims=True))
             raised = raised.astype(BF16)
-            e_ref[head] = raised
+            e_ref[head, rows, :] = raised
             blended.append(dot(raised, values))
         share = jnp.where(here, shares[0], shares[1])
-        r_ref[...] = share
-        o_ref[...] = (jnp.where(here, blended[0], blended[1]) * share).astype(BF16)
+        r_ref[rows, :] = share
+        o_ref[rows, :] = (jnp.where(here, blended[0], blended[1]) * share).astype(BF16)
 
     small = longest(queries) * longest(keys) <= 3600.0
 
     @pl.when(small)
     def _():
-        run(False)
+        run(slice(0, block), block, False)
 
     @pl.when(jnp.logical_not(small))
     def _():
-        run(True)
+        size = 128
+
+        @pl.loop(0, block // size)
+        def _(number):
+            run(aligned(number * size, size, size), size, True)
 
 
 def attend(cell, qkv, spots, pairs, kept=(), block=1024):
@@ -1167,24 +1172,23 @@
         down_got = during(lambda: swap(down_theirs, 1))
         down_parts = add_parts(where, [(down_mine, down_got)], count)
 
-        got, (up_got, out_got, (grads_other, sums_other, qkv_theirs)) = during(
-            lambda: (
-                to_quad(down_parts),
-                during(
-                    lambda: (
-                        swap(up_theirs, 1),
-                        swap(out_theirs, 1),
-                        attend_back(
-                            where, qkv, grad_mixed, mixed, shares, raised, attn_in_t, True
-                        ),
-                    )
-                ),
+        def stage():
+            up_got, out_got, back = during(
+                lambda: (
+                    swap(up_theirs, 1),
+                    swap(out_theirs, 1),
+                    attend_back(where, qkv, grad_mixed, mixed, shares, raised, attn_in_t, True),
+                )
             )
+            return back, add_parts(where, [(out_mine, out_got), (up_mine, up_got)], count)
+
+        got, ((grads_other, sums_other, qkv_theirs), two_parts) = during(
+            lambda: (to_quad(down_parts), during(stage))
         )
-        two_parts = add_parts(where, [(out_mine, out_got), (up_mine, up_got)], count)
-        down_near, down_far = quad_pairs(where, [down_parts[0]] + got, count)
+        down_all = [down_parts[0]] + got
 
         def stage():
+            down_near, down_far = quad_pairs(where, down_all, count)
             got, far, (grads_mine, sums_mine, mine) = during(
                 lambda: (
                     swap(qkv_theirs, 1),

time: 385 us -> 374 us (0.971); the launches traced: 385 us -> 367 us
  loops' own time: 19.2 us -> 9.66 us
  waiting for transfers between devices: 90.1 us -> 81.3 us
    another operation x36 -> x37, loops' own time: 19.2 us -> 9.66 us  [during(): return lax.cond(live, run, blank)]
    ppermute x58, waiting for transfers between devices: 61 us -> 52.6 us  [swap(): return lax.ppermute(value, 'dp', [(i, i ^ mask) for i in range(dp_size)])]
  transfers between devices with their start and end apart: 73 -> 73, of which waited for: 32 -> 33; matrix products, arithmetic and copies ran while one was open for 0% -> 0% of each run, Pallas kernels for 50% -> 53%
where the time goes in v1:
time: 374 us; the launch traced here: 367 us
  Pallas kernels  199 us (53%)
  waiting for transfers between devices  81.3 us (22%)
  starting transfers between devices  59.7 us (16%)
  between operations  14.7 us (4%)
  loops' own time  9.66 us (3%)
    pallas_call x1, Pallas kernels, feed(): call(partial(feed_kernel, count), 'feed', (seq // block,), [SCALARS, row(...  59.7 us
    ppermute x58, waiting for transfers between devices, swap(): return lax.ppermute(value, 'dp', [(i, i ^ mask) for i in range(dp_size)])  52.6 us
    ppermute x58, starting transfers between devices, swap(): return lax.ppermute(value, 'dp', [(i, i ^ mask) for i in range(dp_size)])  41.1 us
    pallas_call x2, Pallas kernels, attend_back(): call(attend_back_kernel, 'attend_back', (pairs, seq // block), [pl.BlockS...  38.6 us
    pallas_call x3, Pallas kernels, attend(): call(attend_kernel, 'attend', (2, seq // block), [SCALARS, SCALARS, SCALA...  28.2 us
    ppermute x12, waiting for transfers between devices, turn(): return lax.ppermute(value, 'fsdp', [(i, i ^ step) for i in range(count)])  18.7 us
    ppermute x12, starting transfers between devices, turn(): return lax.ppermute(value, 'fsdp', [(i, i ^ step) for i in range(count)])  18.5 us
    pallas_call x3, Pallas kernels, outer_call(): call(kernel, name, grid, in_specs, out_specs, out_shape, scratch, 1)  12.9 us
  transfers between devices with their start and end apart: 73, of which 33 were waited for; matrix products, arithmetic and copies ran while one was open for 0% of the time, Pallas kernels for 53%

profile of v1, /device:TPU:0, one launch (start us, length us, event | category | flops | bytes accessed | tf_op | source)
XLA Modules:
  0.0 366.5 jit_solution(1392536047157533698)
XLA Ops:
  10.6 17.7 %conditional.37 = (bf16[64,1152]{1,0:T(8,128)(2,1)}, bf16[64,1152]{1,0:T(8,128)(2,1)}, bf16[64,1152]{1,0:T(8,128)(2,1)}, s32[288,128]{1,0:T(8,128)S(1)}) conditional(s32[]{:T(128)} %convert_element_type.56, () %tuple.315, (bf16[64,1152]{1,0:T(8,128)(2,1)S(1)}, s32[4]{0:T(128)S(1)}, s32[32]{0:T(128)S(1)}, s32[32]{0:T(128)S(1)}, ...), branch_computations={%region_0.0_spmd, %region_1.0_spmd} | conditional | flops 1024 | bytes 1770648 | solution.py:1092
  29.6 39.0 %conditional.38 = (bf16[4,240,768]{2,1,0:T(8,128)(2,1)}, bf16[1024,768]{1,0:T(8,128)(2,1)}, bf16[768,1024]{1,0:T(8,128)(2,1)}, f32[8,768]{1,0:T(8,128)}, f32[1,3...) conditional(s32[]{:T(128)} %convert_element_type.56, () %tuple.318, ...), branch_computations={%region_2.0_spmd, %region_3.0_spmd} | conditional | flops 3075 | bytes 51620072 | solution.py:1092
  30.3 30.0 %conditional.4 = (bf16[1024,768]{1,0:T(8,128)(2,1)}, bf16[768,1024]{1,0:T(8,128)(2,1)}, f32[8,768]{1,0:T(8,128)}, f32[1,3072]{1,0:T(1,128)}, f32[1,2304]{1,0:T(1...) conditional(s32[]{:T(128)} %convert_element_type.24, () %tuple.189, ...), branch_computations={%region_4.0_spmd, %region_5.0_spmd} | conditional | flops 3074 | bytes 46090204 | solution.py:1092
  40.6 18.7 %conditional.3 = (bf16[3,48,768]{2,1,0:T(8,128)(2,1)}, bf16[3,48,768]{2,1,0:T(8,128)(2,1)}, bf16[3,48,768]{2,1,0:T(8,128)(2,1)}, bf16[1024,2304]{1,0:T(8,128)(2,...) conditional(s32[]{:T(128)} %convert_element_type.20, () %tuple.184, ...), branch_computations={%region_10.0_spmd, %region_11.0_spmd} | conditional | flops 2049 | bytes 40796528 | solution.py:1092
  44.1 14.9 %conditional = (bf16[1024,2304]{1,0:T(8,128)(2,1)}, bf16[768,2304]{1,0:T(8,128)(2,1)}, bf16[1024,768]{1,0:T(8,128)(2,1)}, bf16[12,1024,1024]{2,1,0:T(8,128)(2,1)}, f32[1024,768]{1,0:T(8,128)}) conditional(s32[]{:T(128)} %convert_element_type.19, () %tuple.179, (s32[4]{0:T(128)S(1)}, bf16[1024,768]{1,0:T(8,128)(2,1)}, f32[1,2304]{1,0:T(1,128)}, ...), branch_computations={%region_12.0_spmd, %region_13.0_spmd} | conditional | flops 2048 | bytes 38142004 | solution.py:1092
  70.8 31.2 %conditional.39 = (bf16[3,144,768]{2,1,0:T(8,128)(2,1)}, bf16[3,144,768]{2,1,0:T(8,128)(2,1)}, bf16[3,144,768]{2,1,0:T(8,128)(2,1)}, bf16[1024,2304]{1,0:T(8,128...) conditional(s32[]{:T(128)} %convert_element_type.56, () %tuple.320, ...), branch_computations={%region_14.0_spmd, %region_15.0_spmd} | conditional | flops 2050 | bytes 46104960 | solution.py:1092
  74.3 21.2 %conditional.7 = (bf16[1024,2304]{1,0:T(8,128)(2,1)}, bf16[768,2304]{1,0:T(8,128)(2,1)}, bf16[1024,768]{1,0:T(8,128)(2,1)}, bf16[12,1024,1024]{2,1,0:T(8,128)(2,1)}, f32[1024,768]{1,0:T(8,128)}) conditional(s32[]{:T(128)} %convert_element_type.29, () %tuple.203, (pred[]{:T(512)}, bf16[3,48,768]{2,1,0:T(8,128)(2,1)S(1)}, ...), branch_computations={%region_16.0_spmd, %region_17.0_spmd} | conditional | flops 2049 | bytes 38142004 | solution.py:1092
  102.0 22.9 %conditional.40 = (bf16[3,96,768]{2,1,0:T(8,128)(2,1)}, bf16[3,96,768]{2,1,0:T(8,128)(2,1)}, bf16[3,96,768]{2,1,0:T(8,128)(2,1)}, bf16[3,144,768]{2,1,0:T(8,128)...) conditional(s32[]{:T(128)} %convert_element_type.56, () %tuple.317, ...), branch_computations={%region_22.0_spmd, %region_23.0_spmd} | conditional | flops 1025 | bytes 41828792 | solution.py:1092
  129.1 60.5 %conditional.42 = (s32[288,128]{1,0:T(8,128)}, f32[1024,768]{1,0:T(8,128)}, bf16[1024,768]{1,0:T(8,128)(2,1)S(1)}, f32[1,3072]{1,0:T(1,128)S(1)}, f32[8,768]{1,0...) conditional(s32[]{:T(128)} %convert_element_type.56, () %tuple.314, ...), branch_computations={%region_30.0_spmd, %region_31.0_spmd} | conditional | flops 37888 | bytes 17092736 | solution.py:1092
  129.9 59.7 %feed.1 = (bf16[1024,768]{1,0:T(8,128)(2,1)}, f32[1024,768]{1,0:T(8,128)}, bf16[1024,768]{1,0:T(8,128)(2,1)S(1)}, f32[1,3072]{1,0:T(1,128)S(1)}, f32[8,768]{1,0:...) custom-call(s32[4]{0:T(128)S(1)} %get-tuple-element.1027.where, ...), custom_call_target="tpu_custom_call" | custom-call | flops 1024 | bytes 1024 | tf_op jit(solution)/shard_map/cond/branch_1_fun/feed/pallas_call | solution.py:596
  189.6 168.7 %conditional.43 = (f32[192]{0:T(256)}, f32[192]{0:T(256)}, f32[192]{0:T(256)}, f32[192]{0:T(256)}, f32[192]{0:T(256)}, /*index=5*/f32[192]{0:T(256)}, f32[192]{0...) conditional(s32[]{:T(128)} %convert_element_type.56, () %tuple.326, ...), branch_computations={%region_33.0_spmd, %region_34.0_spmd} | conditional | flops 68619 | bytes 75543696 | solution.py:1092
  190.6 166.2 %conditional.29 = (f32[192]{0:T(256)}, f32[192]{0:T(256)}, f32[192]{0:T(256)}, f32[192]{0:T(256)}, f32[192]{0:T(256)}, /*index=5*/f32[192]{0:T(256)}, f32[192]{0...) conditional(s32[]{:T(128)} %convert_element_type.53, () %tuple.295, ...), branch_computations={%region_35.0_spmd, %region_36.74_spmd} | conditional | flops 31754 | bytes 74658616 | solution.py:1092
  199.9 30.2 %conditional.21 = (bf16[4,96,768]{2,1,0:T(8,128)(2,1)}, bf16[4,96,768]{2,1,0:T(8,128)(2,1)}, bf16[4,96,768]{2,1,0:T(8,128)(2,1)}, bf16[1024,1152]{1,0:T(8,128)(2...) conditional(s32[]{:T(128)} %convert_element_type.52, () %tuple.279, ...), branch_computations={%region_39.0_spmd, %region_40.43_spmd} | conditional | flops 2050 | bytes 18876970 | solution.py:1092
  203.4 24.7 %conditional.11 = (bf16[1024,1152]{1,0:T(8,128)(2,1)}, f32[1,1152]{1,0:T(1,128)}, bf16[768,1152]{1,0:T(8,128)(2,1)}, bf16[4,48,1920]{2,1,0:T(8,128)(2,1)}, bf16[...) conditional(s32[]{:T(128)} %convert_element_type.39, () %tuple.229, ...), branch_computations={%region_41.39_spmd, %region_42.42_spmd} | conditional | flops 2049 | bytes 11798781 | solution.py:1092
  203.4 19.8 %conditional.10 = (bf16[768,1536]{1,0:T(8,128)(2,1)}, bf16[768,384]{1,0:T(8,128)(2,1)}, bf16[1024,1152]{1,0:T(8,128)(2,1)}, f32[1,1152]{1,0:T(1,128)}, bf16[768,1152]{1,0:T(8,128)(2,1)}) conditional(s32[]{:T(128)} %convert_element_type.36, () %tuple.226, (bf16[768,1536]{1,0:T(8,128)(2,1)}, bf16[768,384]{1,0:T(8,128)(2,1)}, s32[4]{0:T(128)S(1)}, ...), branch_computations={%region_43.40_spmd, %region_44.0_spmd} | conditional | flops 1024 | bytes 11797624 | solution.py:1092
  203.9 19.3 %attend_back.2 = (bf16[1024,1152]{1,0:T(8,128)(2,1)}, f32[1,1152]{1,0:T(1,128)}, bf16[768,1152]{1,0:T(8,128)(2,1)}) custom-call(s32[4]{0:T(128)S(1)} %get-tuple-element.1065.where, bf16[1024,2304]{1,0:T(8,128)(2,1)} %get-tuple-element.1066.q_ref.k_ref.v_ref, bf16[1024,2304]{1,0:T(8,128)(2,1)} %get-tuple-element.1066.q_ref.k_ref.v_ref, ...), custom_call_target="tpu_custom_call" | custom-call | flops 1024 | bytes 1024 | tf_op jit(solution)/shard_map/cond/branch_1_fun/cond/branch_1_fun/cond/branch_1_fun/cond/branch_1_fun/cond/branch_1_fun/attend_back/pallas_call | solution.py:684
  230.1 38.5 %conditional.22 = (bf16[4,48,1920]{2,1,0:T(8,128)(2,1)}, bf16[4,48,1920]{2,1,0:T(8,128)(2,1)}, bf16[4,48,1920]{2,1,0:T(8,128)(2,1)}, bf16[4,48,1152]{2,1,0:T(8,1...) conditional(s32[]{:T(128)} %convert_element_type.52, () %tuple.278, ...), branch_computations={%region_45.44_spmd, %region_46.49_spmd} | conditional | flops 4098 | bytes 17109570 | solution.py:1092
  233.6 29.2 %conditional.13 = (bf16[4,48,1152]{2,1,0:T(8,128)(2,1)}, bf16[4,48,1152]{2,1,0:T(8,128)(2,1)}, bf16[4,48,1152]{2,1,0:T(8,128)(2,1)}, bf16[4,48,1152]{2,1,0:T(8,1...) conditional(s32[]{:T(128)} %convert_element_type.41, () %tuple.239, ...), branch_computations={%region_47.45_spmd, %region_48.48_spmd} | conditional | flops 4097 | bytes 8261893 | solution.py:1092
  236.1 20.8 %conditional.12 = (bf16[768,1152]{1,0:T(8,128)(2,1)}, bf16[2,96,768]{2,1,0:T(8,128)(2,1)}, bf16[1024,1152]{1,0:T(8,128)(2,1)}, f32[1,1152]{1,0:T(1,128)}, bf16[768,1152]{1,0:T(8,128)(2,1)}) conditional(s32[]{:T(128)} %convert_element_type.40, () %tuple.236, (bf16[768,1152]{1,0:T(8,128)(2,1)}, bf16[2,96,768]{2,1,0:T(8,128)(2,1)S(1)}, ...), branch_computations={%region_49.46_spmd, %region_50.0_spmd} | conditional | flops 1024 | bytes 8258680 | solution.py:1092
  237.6 19.3 %attend_back.3 = (bf16[1024,1152]{1,0:T(8,128)(2,1)}, f32[1,1152]{1,0:T(1,128)}, bf16[768,1152]{1,0:T(8,128)(2,1)}) custom-call(s32[4]{0:T(128)S(1)} %get-tuple-element.1120.where, bf16[1024,2304]{1,0:T(8,128)(2,1)} %get-tuple-element.1121.q_ref.k_ref.v_ref, bf16[1024,2304]{1,0:T(8,128)(2,1)} %get-tuple-element.1121.q_ref.k_ref.v_ref, ...), custom_call_target="tpu_custom_call" | custom-call | flops 1024 | bytes 1024 | tf_op jit(solution)/shard_map/cond/branch_1_fun/cond/branch_1_fun/cond/branch_1_fun/cond/branch_1_fun/cond/branch_1_fun/attend_back/pallas_call | solution.py:684
  268.6 35.0 %conditional.23 = (bf16[4,48,1152]{2,1,0:T(8,128)(2,1)}, bf16[4,48,1152]{2,1,0:T(8,128)(2,1)}, bf16[4,48,1152]{2,1,0:T(8,128)(2,1)}, bf16[240,768]{1,0:T(8,128)(...) conditional(s32[]{:T(128)} %convert_element_type.52, () %tuple.277, (bf16[4,48,1152]{2,1,0:T(8,128)(2,1)}, ...), branch_computations={%region_51.50_spmd, %region_52.57_spmd} | conditional | flops 5122 | bytes 8385116 | solution.py:1092
  272.2 31.4 %conditional.16 = (bf16[240,768]{1,0:T(8,128)(2,1)}, f32[16,768]{1,0:T(8,128)}, bf16[1,1024,768]{2,1,0:T(8,128)(2,1)}) conditional(s32[]{:T(128)} %convert_element_type.46, () %tuple.253, (pred[]{:T(512)}, s32[4]{0:T(128)S(1)}, bf16[4,48,1920]{2,1,0:T(8,128)(2,1)}, bf16[4,48,1920]{2,1,0:T(8,128)(2,1)}, bf16[4,48,1920]{2,1,0:T(8,128)(2,1)}, ...), branch_computations={%region_53.51_spmd, %region_54.56_spmd} | conditional | flops 5121 | bytes 3076383 | solution.py:1092
  305.7 13.8 %conditional.24 = (bf16[48,1152]{1,0:T(8,128)(2,1)}, bf16[48,1152]{1,0:T(8,128)(2,1)}, bf16[48,1152]{1,0:T(8,128)(2,1)}, bf16[240,768]{1,0:T(8,128)(2,1)}, bf16[240,768]{1,0:T(8,128)(2,1)}) conditional(s32[]{:T(128)} %convert_element_type.52, () %tuple.285, (bf16[48,1152]{1,0:T(8,128)(2,1)S(1)}, bf16[48,1152]{1,0:T(8,128)(2,1)S(1)}, ...), branch_computations={%region_59.58_spmd, %region_60.61_spmd} | conditional | flops 1 | bytes 4276485 | solution.py:1092
  320.6 15.2 %conditional.25 = (bf16[48,1152]{1,0:T(8,128)(2,1)}, bf16[48,1152]{1,0:T(8,128)(2,1)}, bf16[48,1152]{1,0:T(8,128)(2,1)}, bf16[240,768]{1,0:T(8,128)(2,1)}, f32[16,768]{1,0:T(8,128)}) conditional(s32[]{:T(128)} %convert_element_type.52, () %tuple.284, (bf16[48,1152]{1,0:T(8,128)(2,1)S(1)}, pred[]{:T(512)}, bf16[240,768]{1,0:T(8,128)(2,1)}, ...), branch_computations={%region_63.62_spmd, %region_64.65_spmd} | conditional | flops 1 | bytes 2998549 | solution.py:1092
  (215 shorter events, 346.1 us)
Async XLA Ops:
  29.6 38.7 %all-gather.3.cloned.1.call-start = ((), (), s32[]{:S(2)}) async-start(), calls=%async_computation | async-start | bytes 1843200 | tf_op jit(solution)/shard_map/cond/branch_1_fun/all_gather | solution.py:1137
  40.6 18.4 %collective-permute-start.12 = (bf16[3,48,768]{2,1,0:T(8,128)(2,1)S(1)}, bf16[3,48,768]{2,1,0:T(8,128)(2,1)}, u32[]{:S(2)}, u32[]{:S(2)}) collective-permute-start(bf16[3,48,768]{2,1,0:T(8,128)(2,1)S(1)} %get-tuple-element.848), channel_id=1, source_target_pairs={{0,24},{4,28},{8,16},{12,20},{16,8},{20,12},{24,0},{28,4},{1,25},{... | collective-permute-start | bytes 663560 | tf_op jit(solution)/shard_map/cond/branch_1_fun/cond/branch_1_fun/cond/branch_1_fun/ppermute | solution.py:1052
  42.2 16.7 %collective-permute-start.11 = (bf16[3,48,768]{2,1,0:T(8,128)(2,1)S(1)}, bf16[3,48,768]{2,1,0:T(8,128)(2,1)}, u32[]{:S(2)}, u32[]{:S(2)}) collective-permute-start(bf16[3,48,768]{2,1,0:T(8,128)(2,1)S(1)} %get-tuple-element.848), channel_id=1, source_target_pairs={{0,16},{4,20},{8,24},{12,28},{16,0},{20,4},{24,8},{28,12},{1,17},{... | collective-permute-start | bytes 663560 | tf_op jit(solution)/shard_map/cond/branch_1_fun/cond/branch_1_fun/cond/branch_1_fun/ppermute | solution.py:1052
  70.8 24.7 %collective-permute-start.19 = (bf16[3,144,768]{2,1,0:T(8,128)(2,1)S(1)}, bf16[3,144,768]{2,1,0:T(8,128)(2,1)}, u32[]{:S(2)}, u32[]{:S(2)}) collective-permute-start(bf16[3,144,768]{2,1,0:T(8,128)(2,1)S(1)} %get-tuple-element.964), channel_id=1, source_target_pairs={{0,24},{4,28},{8,16},{12,20},{16,8},{20,12},{24,0},{28,4},{1,25},{... | collective-permute-start | bytes 1990664 | tf_op jit(solution)/shard_map/cond/branch_1_fun/ppermute | solution.py:1052
  73.2 28.7 %collective-permute-start.18 = (bf16[3,144,768]{2,1,0:T(8,128)(2,1)S(1)}, bf16[3,144,768]{2,1,0:T(8,128)(2,1)}, u32[]{:S(2)}, u32[]{:S(2)}) collective-permute-start(bf16[3,144,768]{2,1,0:T(8,128)(2,1)S(1)} %get-tuple-element.964), channel_id=1, source_target_pairs={{0,16},{4,20},{8,24},{12,28},{16,0},{20,4},{24,8},{28,12},{1,17},{... | collective-permute-start | bytes 1990664 | tf_op jit(solution)/shard_map/cond/branch_1_fun/ppermute | solution.py:1052
  73.8 28.2 %collective-permute-start.17 = (bf16[3,144,768]{2,1,0:T(8,128)(2,1)S(1)}, bf16[3,144,768]{2,1,0:T(8,128)(2,1)}, u32[]{:S(2)}, u32[]{:S(2)}) collective-permute-start(bf16[3,144,768]{2,1,0:T(8,128)(2,1)S(1)} %get-tuple-element.964), channel_id=1, source_target_pairs={{0,8},{4,12},{8,0},{12,4},{16,24},{20,28},{24,16},{28,20},{1,9},{5... | collective-permute-start | bytes 1990664 | tf_op jit(solution)/shard_map/cond/branch_1_fun/ppermute | solution.py:1052
  102.0 17.5 %collective-permute-start.26 = (bf16[3,96,768]{2,1,0:T(8,128)(2,1)}, bf16[3,96,768]{2,1,0:T(8,128)(2,1)}, u32[]{:S(2)}, u32[]{:S(2)}) collective-permute-start(bf16[3,96,768]{2,1,0:T(8,128)(2,1)} %get-tuple-element.1002), channel_id=1, source_target_pairs={{0,24},{4,28},{8,16},{12,20},{16,8},{20,12},{24,0},{28,4},{1,25},{... | collective-permute-start | bytes 1327112 | tf_op jit(solution)/shard_map/cond/branch_1_fun/ppermute | solution.py:1052
  103.7 21.0 %collective-permute-start.25 = (bf16[3,96,768]{2,1,0:T(8,128)(2,1)}, bf16[3,96,768]{2,1,0:T(8,128)(2,1)}, u32[]{:S(2)}, u32[]{:S(2)}) collective-permute-start(bf16[3,96,768]{2,1,0:T(8,128)(2,1)} %get-tuple-element.1002), channel_id=1, source_target_pairs={{0,16},{4,20},{8,24},{12,28},{16,0},{20,4},{24,8},{28,12},{1,17},{... | collective-permute-start | bytes 1327112 | tf_op jit(solution)/shard_map/cond/branch_1_fun/ppermute | solution.py:1052
  104.9 19.9 %collective-permute-start.24 = (bf16[3,96,768]{2,1,0:T(8,128)(2,1)}, bf16[3,96,768]{2,1,0:T(8,128)(2,1)}, u32[]{:S(2)}, u32[]{:S(2)}) collective-permute-start(bf16[3,96,768]{2,1,0:T(8,128)(2,1)} %get-tuple-element.1002), channel_id=1, source_target_pairs={{0,8},{4,12},{8,0},{12,4},{16,24},{20,28},{24,16},{28,20},{1,9},{5... | collective-permute-start | bytes 1327112 | tf_op jit(solution)/shard_map/cond/branch_1_fun/ppermute | solution.py:1052
  129.1 60.5 %all-reduce.3.cloned.1.call-start = ((), (), s32[]{:S(2)}) async-start(), calls=%async_computation.1 | async-start | bytes 294912 | tf_op jit(solution)/shard_map/cond/branch_1_fun/psum | solution.py:1162
  189.8 167.0 %all-reduce.5.cloned.1.call-start = ((), (), s32[]{:S(2)}) async-start(), calls=%async_computation.2 | async-start | bytes 294912 | tf_op jit(solution)/shard_map/cond/branch_1_fun/psum | solution.py:1267
  199.9 28.2 %collective-permute-start.34 = (bf16[4,96,768]{2,1,0:T(8,128)(2,1)}, bf16[4,96,768]{2,1,0:T(8,128)(2,1)}, u32[]{:S(2)}, u32[]{:S(2)}) collective-permute-start(bf16[4,96,768]{2,1,0:T(8,128)(2,1)} %get-tuple-element.1096), channel_id=1, source_target_pairs={{0,8},{4,12},{8,0},{12,4},{16,24},{20,28},{24,16},{28,20},{1,9},{5... | collective-permute-start | bytes 1769480 | tf_op jit(solution)/shard_map/cond/branch_1_fun/cond/branch_1_fun/cond/branch_1_fun/ppermute | solution.py:1052
  201.3 28.8 %collective-permute-start.35 = (bf16[4,96,768]{2,1,0:T(8,128)(2,1)}, bf16[4,96,768]{2,1,0:T(8,128)(2,1)}, u32[]{:S(2)}, u32[]{:S(2)}) collective-permute-start(bf16[4,96,768]{2,1,0:T(8,128)(2,1)} %get-tuple-element.1097), channel_id=1, source_target_pairs={{0,16},{4,20},{8,24},{12,28},{16,0},{20,4},{24,8},{28,12},{1,17},{... | collective-permute-start | bytes 1769480 | tf_op jit(solution)/shard_map/cond/branch_1_fun/cond/branch_1_fun/cond/branch_1_fun/ppermute | solution.py:1052
  201.9 28.2 %collective-permute-start.36 = (bf16[4,96,768]{2,1,0:T(8,128)(2,1)}, bf16[4,96,768]{2,1,0:T(8,128)(2,1)}, u32[]{:S(2)}, u32[]{:S(2)}) collective-permute-start(bf16[4,96,768]{2,1,0:T(8,128)(2,1)} %get-tuple-element.1098), channel_id=1, source_target_pairs={{0,24},{4,28},{8,16},{12,20},{16,8},{20,12},{24,0},{28,4},{1,25},{... | collective-permute-start | bytes 1769480 | tf_op jit(solution)/shard_map/cond/branch_1_fun/cond/branch_1_fun/cond/branch_1_fun/ppermute | solution.py:1052
  203.4 19.8 %collective-permute-start.32 = (bf16[768,1536]{1,0:T(8,128)(2,1)}, bf16[768,1536]{1,0:T(8,128)(2,1)}, u32[]{:S(2)}, u32[]{:S(2)}) collective-permute-start(bf16[768,1536]{1,0:T(8,128)(2,1)} %get-tuple-element.1063), channel_id=1, source_target_pairs={{0,4},{4,0},{8,12},{12,8},{16,20},{20,16},{24,28},{28,24},{1,5},{5... | collective-permute-start | bytes 7077896 | tf_op jit(solution)/shard_map/cond/branch_1_fun/cond/branch_1_fun/cond/branch_1_fun/cond/branch_1_fun/cond/branch_1_fun/ppermute | solution.py:1052
  203.4 19.8 %collective-permute-start.33 = (bf16[768,384]{1,0:T(8,128)(2,1)}, bf16[768,384]{1,0:T(8,128)(2,1)}, u32[]{:S(2)}, u32[]{:S(2)}) collective-permute-start(bf16[768,384]{1,0:T(8,128)(2,1)} %get-tuple-element.1064), channel_id=1, source_target_pairs={{0,4},{4,0},{8,12},{12,8},{16,20},{20,16},{24,28},{28,24},{1,5},{5... | collective-permute-start | bytes 1769480 | tf_op jit(solution)/shard_map/cond/branch_1_fun/cond/branch_1_fun/cond/branch_1_fun/cond/branch_1_fun/cond/branch_1_fun/ppermute | solution.py:1052
  230.1 32.7 %collective-permute-start.39 = (bf16[4,48,1920]{2,1,0:T(8,128)(2,1)}, bf16[4,48,1920]{2,1,0:T(8,128)(2,1)}, u32[]{:S(2)}, u32[]{:S(2)}) collective-permute-start(bf16[4,48,1920]{2,1,0:T(8,128)(2,1)} %get-tuple-element.1156), channel_id=1, source_target_pairs={{0,8},{4,12},{8,0},{12,4},{16,24},{20,28},{24,16},{28,20},{1,9},{5... | collective-permute-start | bytes 2211848 | tf_op jit(solution)/shard_map/cond/branch_1_fun/cond/branch_1_fun/cond/branch_1_fun/ppermute | solution.py:1052
  230.6 32.2 %collective-permute-start.40 = (bf16[4,48,1920]{2,1,0:T(8,128)(2,1)}, bf16[4,48,1920]{2,1,0:T(8,128)(2,1)}, u32[]{:S(2)}, u32[]{:S(2)}) collective-permute-start(bf16[4,48,1920]{2,1,0:T(8,128)(2,1)} %get-tuple-element.1157), channel_id=1, source_target_pairs={{0,16},{4,20},{8,24},{12,28},{16,0},{20,4},{24,8},{28,12},{1,17},{... | collective-permute-start | bytes 2211848 | tf_op jit(solution)/shard_map/cond/branch_1_fun/cond/branch_1_fun/cond/branch_1_fun/ppermute | solution.py:1052
  232.0 32.8 %collective-permute-start.41 = (bf16[4,48,1920]{2,1,0:T(8,128)(2,1)}, bf16[4,48,1920]{2,1,0:T(8,128)(2,1)}, u32[]{:S(2)}, u32[]{:S(2)}) collective-permute-start(bf16[4,48,1920]{2,1,0:T(8,128)(2,1)} %get-tuple-element.1158), channel_id=1, source_target_pairs={{0,24},{4,28},{8,16},{12,20},{16,8},{20,12},{24,0},{28,4},{1,25},{... | collective-permute-start | bytes 2211848 | tf_op jit(solution)/shard_map/cond/branch_1_fun/cond/branch_1_fun/cond/branch_1_fun/ppermute | solution.py:1052
  236.4 20.6 %collective-permute-start.37 = (bf16[768,1152]{1,0:T(8,128)(2,1)}, bf16[768,1152]{1,0:T(8,128)(2,1)}, u32[]{:S(2)}, u32[]{:S(2)}) collective-permute-start(bf16[768,1152]{1,0:T(8,128)(2,1)} %get-tuple-element.1118), channel_id=1, source_target_pairs={{0,4},{4,0},{8,12},{12,8},{16,20},{20,16},{24,28},{28,24},{1,5},{5... | collective-permute-start | bytes 5308424 | tf_op jit(solution)/shard_map/cond/branch_1_fun/cond/branch_1_fun/cond/branch_1_fun/cond/branch_1_fun/cond/branch_1_fun/ppermute | solution.py:1052
  236.4 20.5 %collective-permute-start.38 = (bf16[2,96,768]{2,1,0:T(8,128)(2,1)S(1)}, bf16[2,96,768]{2,1,0:T(8,128)(2,1)}, u32[]{:S(2)}, u32[]{:S(2)}) collective-permute-start(bf16[2,96,768]{2,1,0:T(8,128)(2,1)S(1)} %get-tuple-element.1119), channel_id=1, source_target_pairs={{0,1},{1,0},{2,3},{3,2},{4,5},{5,4},{6,7},{7,6},{8,9},{9,8},{10,11... | collective-permute-start | bytes 884744 | tf_op jit(solution)/shard_map/cond/branch_1_fun/cond/branch_1_fun/cond/branch_1_fun/cond/branch_1_fun/cond/branch_1_fun/ppermute | solution.py:1055
  268.6 34.9 %collective-permute-start.46 = (bf16[4,48,1152]{2,1,0:T(8,128)(2,1)}, bf16[4,48,1152]{2,1,0:T(8,128)(2,1)}, u32[]{:S(2)}, u32[]{:S(2)}) collective-permute-start(bf16[4,48,1152]{2,1,0:T(8,128)(2,1)} %get-tuple-element.1225), channel_id=1, source_target_pairs={{0,8},{4,12},{8,0},{12,4},{16,24},{20,28},{24,16},{28,20},{1,9},{5... | collective-permute-start | bytes 1327112 | tf_op jit(solution)/shard_map/cond/branch_1_fun/cond/branch_1_fun/cond/branch_1_fun/ppermute | solution.py:1052
  269.2 34.4 %collective-permute-start.47 = (bf16[4,48,1152]{2,1,0:T(8,128)(2,1)}, bf16[4,48,1152]{2,1,0:T(8,128)(2,1)}, u32[]{:S(2)}, u32[]{:S(2)}) collective-permute-start(bf16[4,48,1152]{2,1,0:T(8,128)(2,1)} %get-tuple-element.1226), channel_id=1, source_target_pairs={{0,16},{4,20},{8,24},{12,28},{16,0},{20,4},{24,8},{28,12},{1,17},{... | collective-permute-start | bytes 1327112 | tf_op jit(solution)/shard_map/cond/branch_1_fun/cond/branch_1_fun/cond/branch_1_fun/ppermute | solution.py:1052
  270.6 33.0 %collective-permute-start.48 = (bf16[4,48,1152]{2,1,0:T(8,128)(2,1)}, bf16[4,48,1152]{2,1,0:T(8,128)(2,1)}, u32[]{:S(2)}, u32[]{:S(2)}) collective-permute-start(bf16[4,48,1152]{2,1,0:T(8,128)(2,1)} %get-tuple-element.1227), channel_id=1, source_target_pairs={{0,24},{4,28},{8,16},{12,20},{16,8},{20,12},{24,0},{28,4},{1,25},{... | collective-permute-start | bytes 1327112 | tf_op jit(solution)/shard_map/cond/branch_1_fun/cond/branch_1_fun/cond/branch_1_fun/ppermute | solution.py:1052
  (59 other events, 452.0 us)
Sparse Core Ops, SparseCore 0:
  32.6 35.6 all-gather.2
  132.8 33.1 all-reduce.2
  194.1 72.3 all-reduce.4
